TPU v7x, 32 devices: a whole 2x2x4 slice. The times are simulated.
32 devices in a mesh: row: 4 (over y, core), col: 8 (over z, x).
Axes of the slice: x: 2, y: 2, z: 4, core: 2. Of those that a mesh axis runs over, the one named last changes fastest.
Arguments:
- y_blocks: bfloat16 [128, 16, 128, 128], P(('row', 'col')), may hold values from -0.3 to 1.3
- z_blocks: bfloat16 [128, 16, 128, 128], P(('row', 'col')), may hold values from -0.3 to 1.3
- pattern: int32 [128, 16], replicated, may hold values from 0 to 127, as said below
Outputs:
- y_next: bfloat16 [128, 16, 128, 128], P(('row', 'col'))
- z_next: bfloat16 [128, 16, 128, 128], P(('row', 'col'))
Inputs may be any that keep to these rules, and one draw needn't show every extreme that they name: `pattern`: block row i = (8 x + y) * 4 + z belongs to the domain (x, y, z) of a periodic grid of 4 x 8 x 4 domains. It lists 16 distinct block columns, among them i itself; every column is the block row of a domain ((x + a) mod 4, (y + b) mod 8, (z + c) mod 4) with (a, b) one of (0, 0), (1, 0), (-1, 0), (0, 1), (0, -1) and -1 <= c <= 2.
All inputs are finite; a program needn't handle non-finite values.
Results may differ from a plain program's by a relative error of at most 0.0052.
Values may be sent and summed in bfloat16 or wider, within the bound.
No kernel may reach another device: no remote copies, remote signals or barrier semaphores. Data moves between devices by JAX's collectives and lax.ppermute only.
A program may use at most 192 MiB of HBM per device.

v0:
```python
import jax
import jax.numpy as jnp
from jax import lax
from jax.sharding import PartitionSpec as P

neighbour_faces = ((-1, 0), (1, 0), (0, -1), (0, 1))
depth_offsets = (-1, 0, 1, 2)


def from_behind(block, axis, distance):
    devices = range(lax.axis_size(axis))
    route = [((i - distance) % len(devices), i) for i in devices]
    return lax.ppermute(block, axis, route)


def domain_start(coord_x, coord_y, layout):
    row_count, col_count, rows_dev = layout
    return (jnp.mod(coord_x, row_count) * col_count + jnp.mod(coord_y, col_count)) * rows_dev


def domain_offsets(columns, base_x, base_y, layout):
    row_count, col_count, rows_dev = layout
    col_x = columns // (col_count * rows_dev)
    col_y = jnp.mod(columns // rows_dev, col_count)
    diff_x = jnp.mod(col_x - base_x, row_count)
    diff_y = jnp.mod(col_y - base_y, col_count)
    return (
        jnp.where(diff_x == row_count - 1, -1, diff_x),
        jnp.where(diff_y == col_count - 1, -1, diff_y),
    )


def factor_faces_full(stacked):
    return [
        from_behind(stacked, "row", 1),
        from_behind(stacked, "row", -1),
        from_behind(stacked, "col", 1),
        from_behind(stacked, "col", -1),
    ]


def update_faces_full(t_blocks):
    return [
        from_behind(t_blocks, "row", 1),
        from_behind(t_blocks, "row", -1),
        from_behind(t_blocks, "col", 1),
        from_behind(t_blocks, "col", -1),
    ]


def sparse_product(factor, extended, own_cols, window_cols, local_index):
    rows_dev = factor.shape[0]
    slot_count = extended.shape[0] // rows_dev
    candidate_count = slot_count * len(depth_offsets)
    candidate_ids = jnp.arange(candidate_count, dtype=jnp.int32)

    def one_row(inputs):
        factor_row, row_columns, row_local, depth = inputs
        starts = [
            slot_index * rows_dev + jnp.mod(depth + offset, rows_dev)
            for slot_index in range(slot_count)
            for offset in depth_offsets
        ]
        candidates = jnp.concatenate(
            [lax.dynamic_slice_in_dim(extended, start, 1, 0) for start in starts], axis=0
        )
        candidate_cols = jnp.concatenate(
            [lax.dynamic_slice_in_dim(window_cols, start, 1, 0) for start in starts], axis=0
        )
        which = row_local // rows_dev * len(depth_offsets) + jnp.mod(
            jnp.mod(row_local, rows_dev) - depth + 1, rows_dev
        )
        row_pick = which[:, None] == candidate_ids[None, :]
        partner = jnp.einsum(
            "kq,qlbc->klbc",
            row_pick.astype(extended.dtype),
            candidates,
            preferred_element_type=jnp.float32,
        ).astype(extended.dtype)
        partner_cols = jnp.sum(
            jnp.where(row_pick[:, :, None], candidate_cols[None, :, :], 0), axis=1
        )
        lane_pick = (partner_cols[:, None, :] == row_columns[None, :, None]).astype(extended.dtype)
        chosen = jnp.einsum(
            "kml,klbc->kmbc", lane_pick, partner, preferred_element_type=jnp.float32
        ).astype(extended.dtype)
        return jnp.einsum("kab,kmbc->mac", factor_row, chosen, preferred_element_type=jnp.float32)

    return lax.map(one_row, (factor, own_cols, local_index, jnp.arange(rows_dev, dtype=jnp.int32)))


def on_device(y_blocks, z_blocks, pattern):
    rows_dev = y_blocks.shape[0]
    layout = (lax.axis_size("row"), lax.axis_size("col"), rows_dev)
    coord_x = lax.axis_index("row")
    coord_y = lax.axis_index("col")
    first_row = domain_start(coord_x, coord_y, layout)
    own_cols = lax.dynamic_slice_in_dim(pattern, first_row, rows_dev, 0)
    near_cols = [
        lax.dynamic_slice_in_dim(
            pattern,
            domain_start(coord_x + offset_pair[0], coord_y + offset_pair[1], layout),
            rows_dev,
            0,
        )
        for offset_pair in neighbour_faces
    ]
    off_x, off_y = domain_offsets(own_cols, coord_x, coord_y, layout)
    slot = jnp.where(
        off_x == -1,
        1,
        jnp.where(off_x == 1, 2, jnp.where(off_y == -1, 3, jnp.where(off_y == 1, 4, 0))),
    )
    local_index = slot * rows_dev + jnp.mod(own_cols, rows_dev)
    stacked = jnp.stack([y_blocks, z_blocks])
    window_cols = jnp.concatenate([own_cols] + near_cols, axis=0)
    received = factor_faces_full(stacked)
    y_ext = jnp.concatenate([y_blocks] + [piece_blocks[0] for piece_blocks in received], axis=0)
    z_ext = jnp.concatenate([z_blocks] + [piece_blocks[1] for piece_blocks in received], axis=0)
    product = sparse_product(z_blocks, y_ext, own_cols, window_cols, local_index)
    diagonal = own_cols == (first_row + jnp.arange(rows_dev, dtype=jnp.int32))[:, None]
    identity = jnp.eye(y_blocks.shape[2], dtype=jnp.float32)
    t_blocks = (
        1.5 * jnp.where(diagonal[:, :, None, None], identity, jnp.float32(0.0)) - 0.5 * product
    ).astype(jnp.bfloat16)
    t_received = update_faces_full(t_blocks)
    t_ext = jnp.concatenate([t_blocks] + t_received, axis=0)
    y_next = sparse_product(y_blocks, t_ext, own_cols, window_cols, local_index).astype(
        jnp.bfloat16
    )
    z_next = sparse_product(t_blocks, z_ext, own_cols, window_cols, local_index).astype(
        jnp.bfloat16
    )
    return (y_next, z_next)


def solution(mesh):
    in_specs = (P(("row", "col"), None, None, None), P(("row", "col"), None, None, None), P())
    out_specs = (P(("row", "col"), None, None, None), P(("row", "col"), None, None, None))
    return jax.shard_map(
        on_device, mesh=mesh, in_specs=in_specs, out_specs=out_specs, check_vma=False
    )
```

profile of v0, /device:TPU:0, one launch (start us, length us, event | category | flops | bytes accessed | tf_op | source)
XLA Modules:
  0.0 1475.7 jit_solution(1608211550436667072)
XLA Ops:
  20.2 76.5 %collective-permute-done = bf16[2,4,16,128,128]{4,3,2,1,0:T(8,128)(2,1)} collective-permute-done((bf16[2,4,16,128,128]{4,3,2,1,0:T(8,128)(2,1)}, bf16[2,4,16,128,128]{4,3,2,1,0:T(8,128)(2,1)}, u32[]{:S(2)}, u32[]{:S(2)}) %collective-permute-start) | collective-permute-done | bytes 4194336 | tf_op jit(solution)/shard_map/ppermute | solution.py:13
  102.8 87.4 %collective-permute-done.2 = bf16[2,4,16,128,128]{4,3,2,1,0:T(8,128)(2,1)} collective-permute-done((bf16[2,4,16,128,128]{4,3,2,1,0:T(8,128)(2,1)}, bf16[2,4,16,128,128]{4,3,2,1,0:T(8,128)(2,1)}, u32[]{:S(2)}, u32[]{:S(2)}) %collective-permute-start.2) | collective-permute-done | bytes 4194336 | tf_op jit(solution)/shard_map/ppermute | solution.py:13
  203.4 417.4 %while.45 = (s32[]{:T(128)}, f32[4,16,128,128]{3,2,1,0:T(8,128)}, s32[4,16]{1,0:T(4,128)S(1)}, s32[4]{0:T(128)S(1)}, s32[20,16]{0,1:T(8,128)S(1)}, /*index=5*/s3...) while((s32[]{:T(128)}, f32[4,16,128,128]{3,2,1,0:T(8,128)}, ...), condition=%wide.region_2.3_spmd.clone.clone, body=%wide.region_0.2_spmd.clone.sunk.clone | while | flops 1375747072 | bytes 104345480 | solution.py:89
  261.5 15.8 %fusion.168 = bf16[16,16,128,128]{3,0,2,1:T(8,128)(2,1)} fusion(bf16[20,16,128,128]{3,2,1,0:T(8,128)(2,1)} %dynamic-slice_dynamic-update-slice_fusion.199, s32[16]{0:T(128)S(1)} %fusion.167), kind=kOutput, calls=%fused_computation.4.clone.1.clone | convolution fusion | flops 167772480 | bytes 18874432 | tf_op jit(solution)/shard_map/while/body/eval_jaxpr/kq,qlbc->klbc/dot_general | solution.py:74
  277.3 8.9 copy.114
  287.0 12.3 fusion.170
  299.3 12.4 copy.115
  311.7 5.8 fusion.171
  362.1 15.8 %fusion.168 = bf16[16,16,128,128]{3,0,2,1:T(8,128)(2,1)} fusion(bf16[20,16,128,128]{3,2,1,0:T(8,128)(2,1)} %dynamic-slice_dynamic-update-slice_fusion.199, s32[16]{0:T(128)S(1)} %fusion.167), kind=kOutput, calls=%fused_computation.4.clone.1.clone | convolution fusion | flops 167772480 | bytes 18874432 | tf_op jit(solution)/shard_map/while/body/eval_jaxpr/kq,qlbc->klbc/dot_general | solution.py:74
  377.9 8.9 copy.114
  387.6 12.3 fusion.170
  399.9 12.4 copy.115
  412.3 5.8 fusion.171
  462.8 15.8 %fusion.168 = bf16[16,16,128,128]{3,0,2,1:T(8,128)(2,1)} fusion(bf16[20,16,128,128]{3,2,1,0:T(8,128)(2,1)} %dynamic-slice_dynamic-update-slice_fusion.199, s32[16]{0:T(128)S(1)} %fusion.167), kind=kOutput, calls=%fused_computation.4.clone.1.clone | convolution fusion | flops 167772480 | bytes 18874432 | tf_op jit(solution)/shard_map/while/body/eval_jaxpr/kq,qlbc->klbc/dot_general | solution.py:74
  478.6 8.9 copy.114
  488.3 12.3 fusion.170
  500.5 12.4 copy.115
  513.0 5.9 fusion.171
  563.5 15.8 %fusion.168 = bf16[16,16,128,128]{3,0,2,1:T(8,128)(2,1)} fusion(bf16[20,16,128,128]{3,2,1,0:T(8,128)(2,1)} %dynamic-slice_dynamic-update-slice_fusion.199, s32[16]{0:T(128)S(1)} %fusion.167), kind=kOutput, calls=%fused_computation.4.clone.1.clone | convolution fusion | flops 167772480 | bytes 18874432 | tf_op jit(solution)/shard_map/while/body/eval_jaxpr/kq,qlbc->klbc/dot_general | solution.py:74
  579.3 8.9 copy.114
  588.9 12.3 fusion.170
  601.2 12.4 copy.115
  613.6 5.8 fusion.171
  633.6 415.5 %while.47 = (s32[]{:T(128)}, bf16[4,16,128,128]{3,2,1,0:T(8,128)(2,1)}, s32[4,16]{1,0:T(4,128)S(1)}, s32[4]{0:T(128)S(1)}, s32[20,16]{0,1:T(8,128)S(1)}, /*index...) while((s32[]{:T(128)}, ...), condition=%wide.region_8.9_spmd.clone.clone, body=%wide.region_6.8_spmd.clone.sunk.clone | while | flops 1375747072 | bytes 101724040 | solution.py:89
  691.1 15.8 %fusion.190 = bf16[16,16,128,128]{3,0,2,1:T(8,128)(2,1)} fusion(bf16[20,16,128,128]{3,2,1,0:T(8,128)(2,1)} %dynamic-slice_dynamic-update-slice_fusion.239, s32[16]{0:T(128)S(1)} %fusion.189), kind=kOutput, calls=%fused_computation.154.clone.1.clone | convolution fusion | flops 167772480 | bytes 18874432 | tf_op jit(solution)/shard_map/while/body/eval_jaxpr/kq,qlbc->klbc/dot_general | solution.py:74
  706.9 8.9 copy.124
  716.6 12.3 fusion.192
  728.8 12.4 copy.125
  741.3 5.8 fusion.193
  791.4 15.8 %fusion.190 = bf16[16,16,128,128]{3,0,2,1:T(8,128)(2,1)} fusion(bf16[20,16,128,128]{3,2,1,0:T(8,128)(2,1)} %dynamic-slice_dynamic-update-slice_fusion.239, s32[16]{0:T(128)S(1)} %fusion.189), kind=kOutput, calls=%fused_computation.154.clone.1.clone | convolution fusion | flops 167772480 | bytes 18874432 | tf_op jit(solution)/shard_map/while/body/eval_jaxpr/kq,qlbc->klbc/dot_general | solution.py:74
  807.3 8.9 copy.124
  816.9 12.3 fusion.192
  829.2 12.4 copy.125
  841.6 5.8 fusion.193
  891.7 15.8 %fusion.190 = bf16[16,16,128,128]{3,0,2,1:T(8,128)(2,1)} fusion(bf16[20,16,128,128]{3,2,1,0:T(8,128)(2,1)} %dynamic-slice_dynamic-update-slice_fusion.239, s32[16]{0:T(128)S(1)} %fusion.189), kind=kOutput, calls=%fused_computation.154.clone.1.clone | convolution fusion | flops 167772480 | bytes 18874432 | tf_op jit(solution)/shard_map/while/body/eval_jaxpr/kq,qlbc->klbc/dot_general | solution.py:74
  907.5 8.9 copy.124
  917.2 12.3 fusion.192
  929.5 12.4 copy.125
  941.9 5.8 fusion.193
  992.0 15.8 %fusion.190 = bf16[16,16,128,128]{3,0,2,1:T(8,128)(2,1)} fusion(bf16[20,16,128,128]{3,2,1,0:T(8,128)(2,1)} %dynamic-slice_dynamic-update-slice_fusion.239, s32[16]{0:T(128)S(1)} %fusion.189), kind=kOutput, calls=%fused_computation.154.clone.1.clone | convolution fusion | flops 167772480 | bytes 18874432 | tf_op jit(solution)/shard_map/while/body/eval_jaxpr/kq,qlbc->klbc/dot_general | solution.py:74
  1007.8 8.9 copy.124
  1017.5 12.3 fusion.192
  1029.7 12.4 copy.125
  1042.2 5.8 fusion.193
  1060.0 415.4 %while.46 = (s32[]{:T(128)}, bf16[4,16,128,128]{3,2,1,0:T(8,128)(2,1)}, s32[4,16]{1,0:T(4,128)S(1)}, s32[4]{0:T(128)S(1)}, s32[20,16]{0,1:T(8,128)S(1)}, /*index...) while((s32[]{:T(128)}, ...), condition=%wide.region_5.6_spmd.clone.clone, body=%wide.region_3.5_spmd.clone.sunk.clone | while | flops 1375747072 | bytes 101724040 | solution.py:89
  1117.4 15.7 %fusion.179 = bf16[16,16,128,128]{3,0,2,1:T(8,128)(2,1)} fusion(bf16[20,16,128,128]{3,2,1,0:T(8,128)(2,1)} %dynamic-slice_dynamic-update-slice_fusion.219, s32[16]{0:T(128)S(1)} %fusion.178), kind=kOutput, calls=%fused_computation.79.clone.1.clone | convolution fusion | flops 167772480 | bytes 18874432 | tf_op jit(solution)/shard_map/while/body/eval_jaxpr/kq,qlbc->klbc/dot_general | solution.py:74
  1133.1 8.9 copy.119
  1142.8 12.2 fusion.181
  1154.9 12.5 copy.120
  1167.4 5.8 fusion.182
  1217.7 15.7 %fusion.179 = bf16[16,16,128,128]{3,0,2,1:T(8,128)(2,1)} fusion(bf16[20,16,128,128]{3,2,1,0:T(8,128)(2,1)} %dynamic-slice_dynamic-update-slice_fusion.219, s32[16]{0:T(128)S(1)} %fusion.178), kind=kOutput, calls=%fused_computation.79.clone.1.clone | convolution fusion | flops 167772480 | bytes 18874432 | tf_op jit(solution)/shard_map/while/body/eval_jaxpr/kq,qlbc->klbc/dot_general | solution.py:74
  1233.5 8.9 copy.119
  1243.1 12.2 fusion.181
  1255.3 12.5 copy.120
  1267.8 5.8 fusion.182
  1318.1 15.7 %fusion.179 = bf16[16,16,128,128]{3,0,2,1:T(8,128)(2,1)} fusion(bf16[20,16,128,128]{3,2,1,0:T(8,128)(2,1)} %dynamic-slice_dynamic-update-slice_fusion.219, s32[16]{0:T(128)S(1)} %fusion.178), kind=kOutput, calls=%fused_computation.79.clone.1.clone | convolution fusion | flops 167772480 | bytes 18874432 | tf_op jit(solution)/shard_map/while/body/eval_jaxpr/kq,qlbc->klbc/dot_general | solution.py:74
  1333.9 8.9 copy.119
  1343.5 12.2 fusion.181
  1355.7 12.5 copy.120
  1418.5 15.7 %fusion.179 = bf16[16,16,128,128]{3,0,2,1:T(8,128)(2,1)} fusion(bf16[20,16,128,128]{3,2,1,0:T(8,128)(2,1)} %dynamic-slice_dynamic-update-slice_fusion.219, s32[16]{0:T(128)S(1)} %fusion.178), kind=kOutput, calls=%fused_computation.79.clone.1.clone | convolution fusion | flops 167772480 | bytes 18874432 | tf_op jit(solution)/shard_map/while/body/eval_jaxpr/kq,qlbc->klbc/dot_general | solution.py:74
  1434.3 8.9 copy.119
  1443.9 12.2 fusion.181
  1456.1 12.5 copy.120
  1468.6 5.8 fusion.182
  (418 shorter events, 563.4 us)
Async XLA Ops:
  0.6 16.9 %copy-start.3 = (bf16[4,16,128,128]{3,2,1,0:T(8,128)(2,1)S(1)}, bf16[4,16,128,128]{3,2,1,0:T(8,128)(2,1)}, u32[]{:S(2)}) copy-start(bf16[4,16,128,128]{3,2,1,0:T(8,128)(2,1)} %param.9) | copy-start | bytes 6291460
  0.6 15.6 %copy-start.5 = (s32[128,16]{0,1:T(8,128)S(1)}, s32[128,16]{0,1:T(8,128)}, u32[]{:S(2)}) copy-start(s32[128,16]{0,1:T(8,128)} %param.11) | copy-start | bytes 24580
  5.3 91.3 %collective-permute-start = (bf16[2,4,16,128,128]{4,3,2,1,0:T(8,128)(2,1)}, bf16[2,4,16,128,128]{4,3,2,1,0:T(8,128)(2,1)}, u32[]{:S(2)}, u32[]{:S(2)}) collective-permute-start(bf16[2,4,16,128,128]{4,3,2,1,0:T(8,128)(2,1)} %pad_maximum_fusion), channel_id=1, source_target_pairs={{24,0},{0,8},{8,16},{16,24},{25,1},{1,9},{9,17},{17,25},{26,2},{2,... | collective-permute-start | bytes 12582920 | tf_op jit(solution)/shard_map/ppermute | solution.py:13
  5.8 93.9 %collective-permute-start.1 = (bf16[2,4,16,128,128]{4,3,2,1,0:T(8,128)(2,1)}, bf16[2,4,16,128,128]{4,3,2,1,0:T(8,128)(2,1)}, u32[]{:S(2)}, u32[]{:S(2)}) collective-permute-start(bf16[2,4,16,128,128]{4,3,2,1,0:T(8,128)(2,1)} %pad_maximum_fusion), channel_id=1, source_target_pairs={{8,0},{16,8},{24,16},{0,24},{9,1},{17,9},{25,17},{1,25},{10,2},{18... | collective-permute-start | bytes 12582920 | tf_op jit(solution)/shard_map/ppermute | solution.py:13
  7.8 182.4 %collective-permute-start.2 = (bf16[2,4,16,128,128]{4,3,2,1,0:T(8,128)(2,1)}, bf16[2,4,16,128,128]{4,3,2,1,0:T(8,128)(2,1)}, u32[]{:S(2)}, u32[]{:S(2)}) collective-permute-start(bf16[2,4,16,128,128]{4,3,2,1,0:T(8,128)(2,1)} %pad_maximum_fusion), channel_id=1, source_target_pairs={{7,0},{0,1},{1,2},{2,3},{3,4},{4,5},{5,6},{6,7},{15,8},{8,9},{9,10... | collective-permute-start | bytes 12582920 | tf_op jit(solution)/shard_map/ppermute | solution.py:13
  10.1 183.2 %collective-permute-start.3 = (bf16[2,4,16,128,128]{4,3,2,1,0:T(8,128)(2,1)}, bf16[2,4,16,128,128]{4,3,2,1,0:T(8,128)(2,1)}, u32[]{:S(2)}, u32[]{:S(2)}) collective-permute-start(bf16[2,4,16,128,128]{4,3,2,1,0:T(8,128)(2,1)} %pad_maximum_fusion), channel_id=1, source_target_pairs={{1,0},{2,1},{3,2},{4,3},{5,4},{6,5},{7,6},{0,7},{9,8},{10,9},{11,1... | collective-permute-start | bytes 12582920 | tf_op jit(solution)/shard_map/ppermute | solution.py:13
  13.6 1.3 copy-start.2
  196.3 3.8 copy-start
  196.3 7.1 copy-start.1
  203.4 417.4 %copy-start.4 = (f32[128,128]{1,0:T(8,128)S(1)}, f32[128,128]{1,0:T(8,128)}, u32[]{:S(2)}) copy-start(f32[128,128]{1,0:T(8,128)} %fusion.83) | copy-start | bytes 196612
  203.4 417.4 %copy-start.6 = (pred[4,16]{1,0:T(4,128)(4,1)S(1)}, pred[4,16]{1,0:T(4,128)(4,1)}, u32[]{:S(2)}) copy-start(pred[4,16]{1,0:T(4,128)(4,1)} %broadcast_compare_fusion) | copy-start | bytes 196
  626.3 422.8 %collective-permute-start.4 = (bf16[4,16,128,128]{3,2,1,0:T(8,128)(2,1)}, bf16[4,16,128,128]{3,2,1,0:T(8,128)(2,1)S(1)}, u32[]{:S(2)}, u32[]{:S(2)}) collective-permute-start(bf16[4,16,128,128]{3,2,1,0:T(8,128)(2,1)} %get-tuple-element.1234), channel_id=1, source_target_pairs={{24,0},{0,8},{8,16},{16,24},{25,1},{1,9},{9,17},{17,25},{26,2},{2,... | collective-permute-start | bytes 6291464 | tf_op jit(solution)/shard_map/ppermute | solution.py:13
  626.3 424.3 %collective-permute-start.5 = (bf16[4,16,128,128]{3,2,1,0:T(8,128)(2,1)}, bf16[4,16,128,128]{3,2,1,0:T(8,128)(2,1)}, u32[]{:S(2)}, u32[]{:S(2)}) collective-permute-start(bf16[4,16,128,128]{3,2,1,0:T(8,128)(2,1)} %get-tuple-element.1234), channel_id=1, source_target_pairs={{8,0},{16,8},{24,16},{0,24},{9,1},{17,9},{25,17},{1,25},{10,2},{18... | collective-permute-start | bytes 6291464 | tf_op jit(solution)/shard_map/ppermute | solution.py:13
  628.1 425.7 %collective-permute-start.6 = (bf16[4,16,128,128]{3,2,1,0:T(8,128)(2,1)}, bf16[4,16,128,128]{3,2,1,0:T(8,128)(2,1)}, u32[]{:S(2)}, u32[]{:S(2)}) collective-permute-start(bf16[4,16,128,128]{3,2,1,0:T(8,128)(2,1)} %get-tuple-element.1234), channel_id=1, source_target_pairs={{7,0},{0,1},{1,2},{2,3},{3,4},{4,5},{5,6},{6,7},{15,8},{8,9},{9,10... | collective-permute-start | bytes 6291464 | tf_op jit(solution)/shard_map/ppermute | solution.py:13
  630.5 426.4 %collective-permute-start.7 = (bf16[4,16,128,128]{3,2,1,0:T(8,128)(2,1)}, bf16[4,16,128,128]{3,2,1,0:T(8,128)(2,1)}, u32[]{:S(2)}, u32[]{:S(2)}) collective-permute-start(bf16[4,16,128,128]{3,2,1,0:T(8,128)(2,1)} %get-tuple-element.1234), channel_id=1, source_target_pairs={{1,0},{2,1},{3,2},{4,3},{5,4},{6,5},{7,6},{0,7},{9,8},{10,9},{11,1... | collective-permute-start | bytes 6291464 | tf_op jit(solution)/shard_map/ppermute | solution.py:13
where the time goes:
time: 1500 us; the launch traced here: 1480 us
  local copies, waits for them, and re-layouts  774 us (52%)
  matrix products  406 us (27%)
  waiting for transfers between devices  164 us (11%)
  loops' own time  91.4 us (6%)
  other arithmetic  25.1 us (2%)
  starting transfers between devices  15 us (1%)
    while x228, local copies, waits for them, and re-layouts  433 us
    dot_general x12, matrix products, one_row(): jnp.einsum('kq,qlbc->klbc', row_pick.astype(extended.dtype), candidates,...  189 us
    ppermute x8, waiting for transfers between devices, from_behind(): return lax.ppermute(block, axis, route)  164 us
    dot_general x12, local copies, waits for them, and re-layouts, one_row(): jnp.einsum('kml,klbc->kmbc', lane_pick, partner, preferred_element_type=j...  149 us
    dot_general x12, matrix products, one_row(): jnp.einsum('kml,klbc->kmbc', lane_pick, partner, preferred_element_type=j...  147 us
    dot_general x12, local copies, waits for them, and re-layouts, one_row(): jnp.einsum('kq,qlbc->klbc', row_pick.astype(extended.dtype), candidates,...  107 us
    another operation x3, loops' own time, sparse_product(): lax.map(one_row, (factor, own_cols, local_index, jnp.arange(rows_dev, dty...  91.4 us
    dot_general x12, matrix products, one_row(): jnp.einsum('kab,kmbc->mac', factor_row, chosen, preferred_element_type=jn...  69.5 us
  transfers between devices with their start and end apart: 8, of which 2 were waited for; matrix products, arithmetic and copies ran while one was open for 28% of the time, Pallas kernels for 0%

commit v1 on v0

v1 whole, which is shorter than its diff:
```python
import functools

import jax
import jax.numpy as jnp
from jax import lax
from jax.experimental import pallas as pl
from jax.experimental.pallas import tpu as pltpu
from jax.sharding import PartitionSpec as P


HBM = pl.BlockSpec(memory_space=pl.ANY)
SMEM = pl.BlockSpec(memory_space=pltpu.SMEM)
VMEM = pl.BlockSpec(memory_space=pltpu.VMEM)

OWN, PARTNER, BEYOND, UPPER, LOWER = range(5)


def slot_domains(row_count, col_count):
    coord_x = lax.axis_index("row")
    coord_y = lax.axis_index("col")
    step = 1 - 2 * lax.rem(coord_y, 2)
    partner = coord_y + step
    beyond = lax.rem(coord_y - step + col_count, col_count)
    upper = lax.rem(coord_x + 1, row_count)
    lower = lax.rem(coord_x + row_count - 1, row_count)
    return (
        coord_x * col_count + coord_y,
        coord_x * col_count + partner,
        coord_x * col_count + beyond,
        upper * col_count + coord_y,
        lower * col_count + coord_y,
    )


def pack_body(grid, with_tables, pattern, blocks, *refs):
    row_count, col_count = grid
    rows, lanes, size, _ = blocks.shape
    units = refs[:5]
    if with_tables:
        table, near, dense, in_sem, out_sem = refs[5:]
    else:
        dense, in_sem, out_sem = refs[5:]
    domains = slot_domains(row_count, col_count)
    dense[...] = jnp.zeros(dense.shape, dense.dtype)
    if with_tables:
        for i in range(rows * 5 * rows):
            table[i] = -1
    for z in range(rows):
        for k in range(lanes):
            column = pattern[domains[0] * rows + z, k]
            domain = lax.div(column, rows)
            depth = column - domain * rows
            slot = jnp.int32(OWN)
            for other in range(1, 5):
                slot = jnp.where(domain == domains[other], other, slot)
            if with_tables:
                table[(z * 5 + slot) * rows + depth] = k
            pltpu.make_async_copy(
                blocks.at[z, k],
                dense.at[slot, pl.ds(z * size, size), pl.ds(pl.multiple_of(depth * size, size), size)],
                in_sem,
            ).start()
    if with_tables:
        for i in range(5 * rows * rows):
            near[i] = 0

        @pl.loop(0, lanes)
        def _(k):
            for slot in range(1, 5):
                for z in range(rows):
                    column = pattern[domains[slot] * rows + z, k]
                    domain = lax.div(column, rows)
                    place = (slot * rows + z) * rows + column - domain * rows
                    near[place] = jnp.where(domain == domains[0], 1, near[place])

    pltpu.make_async_copy(blocks, blocks, in_sem).wait()
    copies = [
        pltpu.make_async_copy(dense.at[slot], units[slot], out_sem.at[slot]) for slot in range(5)
    ]
    for copy in copies:
        copy.start()
    for copy in copies:
        copy.wait()


def pack(blocks, pattern, grid, with_tables):
    rows, _, size, _ = blocks.shape
    order = rows * size
    shapes = [jax.ShapeDtypeStruct((order, order), blocks.dtype)] * 5
    specs = [HBM] * 5
    if with_tables:
        shapes = shapes + [jax.ShapeDtypeStruct((5 * rows * rows,), jnp.int32)] * 2
        specs = specs + [SMEM] * 2
    return pl.pallas_call(
        functools.partial(pack_body, grid, with_tables),
        out_shape=shapes,
        in_specs=[SMEM, HBM],
        out_specs=specs,
        scratch_shapes=[
            pltpu.VMEM((5, order, order), blocks.dtype),
            pltpu.SemaphoreType.DMA,
            pltpu.SemaphoreType.DMA((5,)),
        ],
    )(pattern, blocks)


class Stage:
    def __init__(self, loads, table, near, sinks, outs, blocks_sem, size):
        self.loads, self.table, self.near = loads, table, near
        self.sinks, self.outs, self.blocks_sem, self.size = sinks, outs, blocks_sem, size
        self.arrived = set()
        self.pending = []

    def load(self, key):
        copy, buffer = self.loads[key]
        if key not in self.arrived:
            copy.wait()
            self.arrived.add(key)
        return buffer[...]

    def dot(self, left, right):
        left = self.load(left) if isinstance(left, str) else left
        right = self.load(right) if isinstance(right, str) else right
        return jnp.dot(left, right, preferred_element_type=jnp.float32)

    def scaled(self, value, present, diagonal=False):
        size = self.size
        rows = value.shape[0] // size
        bands = []
        for z in range(rows):
            band = []
            for depth in range(rows):
                block = value[z * size : (z + 1) * size, depth * size : (depth + 1) * size]
                block = block * jnp.where(present(z, depth), jnp.float32(-0.5), jnp.float32(0.0))
                if diagonal and z == depth:
                    r = lax.broadcasted_iota(jnp.int32, (size, size), 0)
                    c = lax.broadcasted_iota(jnp.int32, (size, size), 1)
                    block = block + jnp.where(r == c, jnp.float32(1.5), jnp.float32(0.0))
                band.append(block)
            bands.append(jnp.concatenate(band, axis=1))
        return jnp.concatenate(bands, axis=0).astype(jnp.bfloat16)

    def own_present(self, slot, rows):
        return lambda z, depth: self.table[(z * 5 + slot) * rows + depth] >= 0

    def near_present(self, slot, rows):
        return lambda z, depth: self.near[(slot * rows + z) * rows + depth] > 0

    def emit(self, sink, slot, staging, value):
        size = self.size
        rows = value.shape[0] // size
        staging[...] = value.astype(staging.dtype)
        target = self.sinks[sink]
        for z in range(rows):
            for depth in range(rows):
                place = self.table[(z * 5 + slot) * rows + depth]
                copy = pltpu.make_async_copy(
                    staging.at[pl.ds(z * size, size), pl.ds(depth * size, size)],
                    target.at[z, jnp.maximum(place, 0)],
                    self.blocks_sem.at[len(self.pending)],
                )

                @pl.when(place >= 0)
                def _(copy=copy):
                    copy.start()

                self.pending.append((place, copy))

    def finish(self):
        for place, copy in self.pending:

            @pl.when(place >= 0)
            def _(copy=copy):
                copy.wait()


def stage_call(body, loads, tables, sinks, outs, sparse_shape, emits, after=()):
    keys, sink_keys, out_keys = list(loads), list(sinks), list(outs)
    known = [key for key in sink_keys if sinks[key] is not None]
    size = sparse_shape.shape[2]
    order = sparse_shape.shape[0] * size
    n_after = len(after)

    def kernel(*refs):
        refs = list(refs)
        take = lambda n: [refs.pop(0) for _ in range(n)]
        sources = take(len(keys))
        table, near = take(2)
        take(len(known))
        take(n_after)
        targets = take(len(sink_keys))
        results = take(len(out_keys))
        buffers = take(len(keys))
        stagings = take(emits)
        in_sem, blocks_sem = take(2)
        pairs = {}
        for i, key in enumerate(keys):
            copy = pltpu.make_async_copy(sources[i], buffers[i], in_sem.at[i])
            copy.start()
            pairs[key] = (copy, buffers[i])
        stage = Stage(
            pairs,
            table,
            near,
            dict(zip(sink_keys, targets)),
            dict(zip(out_keys, results)),
            blocks_sem,
            size,
        )
        body(stage, stagings)
        stage.finish()

    first_sink = len(keys) + 2
    return pl.pallas_call(
        kernel,
        out_shape=[sparse_shape] * len(sink_keys) + [outs[key] for key in out_keys],
        in_specs=[HBM] * len(keys) + [SMEM] * 2 + [HBM] * len(known) + [HBM] * n_after,
        out_specs=[HBM] * len(sink_keys) + [VMEM] * len(out_keys),
        scratch_shapes=[pltpu.VMEM(loads[key].shape, loads[key].dtype) for key in keys]
        + [pltpu.VMEM((order, order), sparse_shape.dtype)] * emits
        + [
            pltpu.SemaphoreType.DMA((len(keys),)),
            pltpu.SemaphoreType.DMA((max(1, emits * sparse_shape.shape[0] ** 2),)),
        ],
        input_output_aliases={
            first_sink + i: sink_keys.index(key) for i, key in enumerate(known)
        },
    )(*[loads[key] for key in keys], *tables, *[sinks[key] for key in known], *after)


def on_device(y_blocks, z_blocks, pattern):
    row_count, col_count = lax.axis_size("row"), lax.axis_size("col")
    rows, _, size, _ = y_blocks.shape
    order = rows * size
    grid = (row_count, col_count)
    swap = [(i, i ^ 1) for i in range(col_count)]
    hop = [(i, (i + 2 - 4 * (i % 2)) % col_count) for i in range(col_count)]
    upward = [(i, (i + 1) % row_count) for i in range(row_count)]
    downward = [(i, (i - 1) % row_count) for i in range(row_count)]

    def move(axis, route, value):
        return lax.ppermute(value, axis, route)

    sparse = jax.ShapeDtypeStruct(y_blocks.shape, y_blocks.dtype)
    unit = jax.ShapeDtypeStruct((order, order), y_blocks.dtype)
    sums = jax.ShapeDtypeStruct((order, order), jnp.float32)

    yo, ya, yb, yp, ym = pack(y_blocks, pattern, grid, False)
    yb_seen = move("col", swap, yb)
    y_po = move("row", downward, ym)
    y_mo = move("row", upward, yp)
    y_ao = move("col", swap, ya)
    (z_in, _) = lax.optimization_barrier((z_blocks, yb))
    zo, za, zb, zp, zm, table, near = pack(z_in, pattern, grid, True)
    tables = (table, near)
    zb_seen = move("col", swap, zb)
    y_aa = move("col", swap, yo)
    z_aa = move("col", swap, zo)
    y_pp, z_pp, z_po = (move("row", downward, yo), move("row", downward, zo), move("row", downward, zm))
    y_mm, z_mm, z_mo = (move("row", upward, yo), move("row", upward, zo), move("row", upward, zp))
    y_bo = move("col", hop, yb_seen)

    def own_body(s, stagings):
        value = s.dot("zo", "yo")
        for left, right in (("zp", "y_po"), ("zm", "y_mo"), ("za", "y_ao"), ("zb", "y_bo")):
            value = value + s.dot(left, right)
        s.outs["t"][...] = s.scaled(value, s.own_present(OWN, rows), True)

    (to,) = stage_call(
        own_body,
        dict(zo=zo, yo=yo, zp=zp, y_po=y_po, zm=zm, y_mo=y_mo, za=za, y_ao=y_ao, zb=zb, y_bo=y_bo),
        tables, {}, dict(t=unit), sparse, 0,
    )
    t_aa = move("col", swap, to)
    z_ao = move("col", swap, lax.optimization_barrier((za, to))[0])
    t_pp = move("row", downward, to)
    t_mm = move("row", upward, to)
    z_bo = move("col", hop, zb_seen)
    y_bb = move("col", hop, y_aa)
    z_bb = move("col", hop, z_aa)
    t_bb = move("col", hop, t_aa)

    def edge_body(slot, first, s, stagings):
        t_od = s.scaled(s.dot("zo", "yd") + s.dot("zd", "y_dd"), s.own_present(slot, rows))
        s.outs["t_od"][...] = t_od
        z_next = s.dot("to", "zd") + s.dot(s.outs["t_od"][...], "z_dd")
        s.emit("z", slot, stagings[0], z_next)
        t_do = s.scaled(s.dot("z_do", "yo") + s.dot("z_dd", "y_do"), s.near_present(slot, rows))
        y_sum = s.dot("yo", "to") if first else s.load("y_sum")
        s.outs["y_sum"][...] = y_sum + s.dot("yd", t_do)
        z_sum = s.dot("to", "zo") if first else s.load("z_sum")
        s.outs["z_sum"][...] = z_sum + s.dot(s.outs["t_od"][...], "z_do")

    def edge(slot, yd, zd, y_dd, y_do, z_dd, z_do, z_sink, so_far):
        loads = dict(zo=zo, yd=yd, zd=zd, y_dd=y_dd, to=to, z_dd=z_dd, z_do=z_do, yo=yo, y_do=y_do)
        if so_far:
            loads.update(y_sum=so_far[0], z_sum=so_far[1])
        return stage_call(
            functools.partial(edge_body, slot, not so_far), loads, tables,
            dict(z=z_sink), dict(t_od=unit, y_sum=sums, z_sum=sums), sparse, 1,
        )

    z_next, t_op, y_sum, z_sum = edge(UPPER, yp, zp, y_pp, y_po, z_pp, z_po, None, ())
    z_next, t_om, y_sum, z_sum = edge(LOWER, ym, zm, y_mm, y_mo, z_mm, z_mo, z_next, (y_sum, z_sum))

    def partner_body(s, stagings):
        t_oa = s.scaled(s.dot("zo", "ya") + s.dot("za", "y_aa"), s.own_present(PARTNER, rows))
        s.outs["t_oa"][...] = t_oa
        s.emit("z", PARTNER, stagings[0], s.dot("to", "za") + s.dot(s.outs["t_oa"][...], "z_aa"))

    z_next, t_oa = stage_call(
        partner_body, dict(zo=zo, ya=ya, za=za, y_aa=y_aa, to=to, z_aa=z_aa),
        tables, dict(z=z_next), dict(t_oa=unit), sparse, 1,
    )

    def outer_body(slots, s, stagings):
        for i, slot in enumerate(slots):
            s.emit("y", slot, stagings[i], s.dot("yo", f"t_o{i}") + s.dot(f"y{i}", f"t{i}"))

    (y_next,) = stage_call(
        functools.partial(outer_body, (UPPER, LOWER)),
        dict(yo=yo, t_o0=t_op, y0=yp, t0=t_pp, t_o1=t_om, y1=ym, t1=t_mm),
        tables, dict(y=None), {}, sparse, 2,
    )
    (y_next,) = stage_call(
        functools.partial(outer_body, (PARTNER,)),
        dict(yo=yo, t_o0=t_oa, y0=ya, t0=t_aa), tables, dict(y=y_next), {}, sparse, 1,
    )
    z_next, t_ob, y_sum, z_sum = edge(BEYOND, yb, zb, y_bb, y_bo, z_bb, z_bo, z_next, (y_sum, z_sum))

    def last_body(s, stagings):
        s.emit("y", BEYOND, stagings[0], s.dot("yo", "t_ob") + s.dot("yb", "t_bb"))
        s.emit("z", OWN, stagings[1], s.load("z_sum") + s.dot("t_oa", "z_ao"))
        t_ao = s.scaled(s.dot("z_ao", "yo") + s.dot("z_aa", "y_ao"), s.near_present(PARTNER, rows))
        s.emit("y", OWN, stagings[2], s.load("y_sum") + s.dot("ya", t_ao))

    y_next, z_next = stage_call(
        last_body,
        dict(yo=yo, t_ob=t_ob, yb=yb, t_bb=t_bb, t_oa=t_oa, z_ao=z_ao, z_sum=z_sum, z_aa=z_aa, y_ao=y_ao, ya=ya, y_sum=y_sum),
        tables, dict(y=y_next, z=z_next), {}, sparse, 3,
    )
    return y_next, z_next


def solution(mesh):
    spec = P(("row", "col"), None, None, None)

    return jax.shard_map(on_device, mesh=mesh, in_specs=(spec, spec, P()), out_specs=(spec, spec), check_vma=False)
```

time: 1500 us -> 136 us (0.09); the launches traced: 1480 us -> 135 us
  local copies, waits for them, and re-layouts: 774 us -> 4.14 us
  matrix products: 406 us -> 0 us
  waiting for transfers between devices: 164 us -> 47.1 us
  loops' own time: 91.4 us -> 0 us
  Pallas kernels: 0 us -> 57.8 us
  other arithmetic: 25.1 us -> 0 us
    while x228 -> x0, local copies, waits for them, and re-layouts: 433 us -> none
    dot_general x36 -> x0, matrix products: 406 us -> none  [the longest x12 189 us: one_row(): jnp.einsum('kq,qlbc->klbc', row_pick.astype(extended.dtype), candidates,...]
    dot_general x24 -> x0, local copies, waits for them, and re-layouts: 256 us -> none  [the longest x12 149 us: one_row(): jnp.einsum('kml,klbc->kmbc', lane_pick, partner, preferred_element_type=j...]
    ppermute x8 -> x22, waiting for transfers between devices: 164 us -> 47.1 us  [move(): return lax.ppermute(value, axis, route)]
    another operation x3 -> x0, loops' own time: 91.4 us -> none  [sparse_product(): lax.map(one_row, (factor, own_cols, local_index, jnp.arange(rows_dev, dty...]
    pallas_call x0 -> x10, Pallas kernels: none -> 57.8 us  [the longest x8 46.9 us: stage_call(): pl.pallas_call(kernel, out_shape=[sparse_shape] * len(sink_keys) + [outs[...]
    concatenate x27 -> x0, local copies, waits for them, and re-layouts: 30.4 us -> none  [the longest x12 22.8 us: one_row(): jnp.concatenate([lax.dynamic_slice_in_dim(extended, start, 1, 0) for star...]
    unnamed x28 -> x31, local copies, waits for them, and re-layouts: 29.2 us -> 4.14 us
  transfers between devices with their start and end apart: 8 -> 22, of which waited for: 2 -> 6; matrix products, arithmetic and copies ran while one was open for 28% -> 0% of each run, Pallas kernels for 0% -> 35%
where the time goes in v1:
time: 136 us; the launch traced here: 135 us
  Pallas kernels  57.8 us (42%)
  waiting for transfers between devices  47.1 us (35%)
  starting transfers between devices  24.5 us (18%)
  local copies, waits for them, and re-layouts  4.14 us (3%)
    ppermute x22, waiting for transfers between devices, move(): return lax.ppermute(value, axis, route)  47.1 us
    pallas_call x8, Pallas kernels, stage_call(): pl.pallas_call(kernel, out_shape=[sparse_shape] * len(sink_keys) + [outs[...  46.9 us
    ppermute x22, starting transfers between devices, move(): return lax.ppermute(value, axis, route)  24.5 us
    pallas_call x2, Pallas kernels, pack(): pl.pallas_call(functools.partial(pack_body, grid, with_tables), out_shape...  11 us
    unnamed x31, local copies, waits for them, and re-layouts  4.14 us
  transfers between devices with their start and end apart: 22, of which 6 were waited for; matrix products, arithmetic and copies ran while one was open for 0% of the time, Pallas kernels for 35%

profile of v1, /device:TPU:0, one launch (start us, length us, event | category | flops | bytes accessed | tf_op | source)
XLA Modules:
  0.0 134.7 jit_solution(16768254946803519745)
XLA Ops:
  0.6 1.4 %copy.11.pattern = s32[128,16]{1,0:T(8,128)} copy(s32[128,16]{0,1:T(8,128)} %param.5) | data formatting | bytes 16384 | tf_op args[2]
  2.1 5.0 %shard_map.50 = (bf16[512,512]{1,0:T(8,128)(2,1)}, bf16[512,512]{1,0:T(8,128)(2,1)}, bf16[512,512]{1,0:T(8,128)(2,1)}, bf16[512,512]{1,0:T(8,128)(2,1)}, bf16[512,512]{1,0:T(8,128)(2,1)}) custom-call(s32[128,16]{1,0:T(8,128)} %copy.11.pattern, bf16[4,16,128,128]{3,2,1,0:T(8,128)(2,1)} %blocks.1), custom_call_target="tpu_custom_call" | custom-call | tf_op jit(solution)/shard_map/pallas_call | solution.py:94
  7.1 3.0 %collective-permute-start.5 = (bf16[512,512]{1,0:T(8,128)(2,1)}, bf16[512,512]{1,0:T(8,128)(2,1)S(1)}, u32[]{:S(2)}, u32[]{:S(2)}) collective-permute-start(bf16[512,512]{1,0:T(8,128)(2,1)} %get-tuple-element.31.refs_1_.refs_2_), channel_id=1, source_target_pairs={{0,1},{1,0},{2,3},{3,2},{4,5},{5,4},{6,7},{7,6},{8,9},{9,8},{10,11... | collective-permute-start | bytes 1572872 | tf_op jit(solution)/shard_map/ppermute | solution.py:242
  10.1 0.1 collective-permute-start.4
  10.2 0.9 collective-permute-start.2
  11.0 0.0 collective-permute-start.3
  11.0 6.0 %shard_map.51 = (bf16[512,512]{1,0:T(8,128)(2,1)}, bf16[512,512]{1,0:T(8,128)(2,1)}, bf16[512,512]{1,0:T(8,128)(2,1)}, bf16[512,512]{1,0:T(8,128)(2,1)}, bf16[51...) custom-call(s32[128,16]{1,0:T(8,128)} %copy.11.pattern, bf16[4,16,128,128]{3,2,1,0:T(8,128)(2,1)} %blocks.2), custom_call_target="tpu_custom_call" | custom-call | tf_op jit(solution)/shard_map/pallas_call | solution.py:94
  17.0 1.8 %collective-permute-start.15 = (bf16[512,512]{1,0:T(8,128)(2,1)}, bf16[512,512]{1,0:T(8,128)(2,1)S(1)}, u32[]{:S(2)}, u32[]{:S(2)}) collective-permute-start(bf16[512,512]{1,0:T(8,128)(2,1)} %get-tuple-element.33.refs_0_), channel_id=1, source_target_pairs={{0,24},{8,0},{16,8},{24,16},{1,25},{9,1},{17,9},{25,17},{2,26},{10... | collective-permute-start | bytes 1572872 | tf_op jit(solution)/shard_map/ppermute | solution.py:242
  18.8 4.3 %collective-permute-done.5 = bf16[512,512]{1,0:T(8,128)(2,1)S(1)} collective-permute-done((bf16[512,512]{1,0:T(8,128)(2,1)}, bf16[512,512]{1,0:T(8,128)(2,1)S(1)}, u32[]{:S(2)}, u32[]{:S(2)}) %collective-permute-start.5) | collective-permute-done | bytes 524320 | tf_op jit(solution)/shard_map/ppermute | solution.py:242
  23.1 0.0 collective-permute-start.16
  23.1 10.4 %collective-permute-done.4.refs_7_.refs_8_ = bf16[512,512]{1,0:T(8,128)(2,1)S(1)} collective-permute-done((bf16[512,512]{1,0:T(8,128)(2,1)}, bf16[512,512]{1,0:T(8,128)(2,1)S(1)}, u32[]{:S(2)}, u32[]{:S(2)}) %collective-permute-start.4) | collective-permute-done | bytes 524320 | tf_op jit(solution)/shard_map/ppermute | solution.py:242
  33.5 0.4 collective-permute-start.14
  33.8 0.0 collective-permute-done.2.refs_3_.refs_8_
  33.8 0.2 collective-permute-start.12
  34.0 0.0 collective-permute-done.3.refs_5_.refs_8_
  34.0 1.7 %collective-permute-start.7 = (bf16[512,512]{1,0:T(8,128)(2,1)}, bf16[512,512]{1,0:T(8,128)(2,1)}, u32[]{:S(2)}, u32[]{:S(2)}) collective-permute-start(bf16[512,512]{1,0:T(8,128)(2,1)} %get-tuple-element.33.refs_0_), channel_id=1, source_target_pairs={{0,1},{1,0},{2,3},{3,2},{4,5},{5,4},{6,7},{7,6},{8,9},{9,8},{10,11... | collective-permute-start | bytes 1572872 | tf_op jit(solution)/shard_map/ppermute | solution.py:242
  35.7 0.0 collective-permute-done.15.refs_5_
  35.7 0.3 collective-permute-start.9
  36.0 0.0 collective-permute-done.16.refs_6_
  36.0 1.8 %collective-permute-start.6 = (bf16[512,512]{1,0:T(8,128)(2,1)S(1)}, bf16[512,512]{1,0:T(8,128)(2,1)S(1)}, u32[]{:S(2)}, u32[]{:S(2)}) collective-permute-start(bf16[512,512]{1,0:T(8,128)(2,1)S(1)} %collective-permute-done.5), channel_id=1, source_target_pairs={{0,2},{1,7},{2,4},{3,1},{4,6},{5,3},{6,0},{7,5},{8,10},{9,15},{10,... | collective-permute-start | bytes 1572872 | tf_op jit(solution)/shard_map/ppermute | solution.py:242
  37.9 7.2 %collective-permute-done.14.refs_3_ = bf16[512,512]{1,0:T(8,128)(2,1)S(1)} collective-permute-done((bf16[512,512]{1,0:T(8,128)(2,1)S(1)}, bf16[512,512]{1,0:T(8,128)(2,1)S(1)}, u32[]{:S(2)}, u32[]{:S(2)}) %collective-permute-start.14) | collective-permute-done | bytes 524320 | tf_op jit(solution)/shard_map/ppermute | solution.py:242
  45.0 3.0 %collective-permute-start.13 = (bf16[512,512]{1,0:T(8,128)(2,1)}, bf16[512,512]{1,0:T(8,128)(2,1)}, u32[]{:S(2)}, u32[]{:S(2)}) collective-permute-start(bf16[512,512]{1,0:T(8,128)(2,1)} %get-tuple-element.35.refs_2_), channel_id=1, source_target_pairs={{0,8},{8,16},{16,24},{24,0},{1,9},{9,17},{17,25},{25,1},{2,10},{10... | collective-permute-start | bytes 1572872 | tf_op jit(solution)/shard_map/ppermute | solution.py:242
  48.0 0.0 collective-permute-done.12.refs_5_
  48.0 1.5 %collective-permute-start = (bf16[512,512]{1,0:T(8,128)(2,1)S(1)}, bf16[512,512]{1,0:T(8,128)(2,1)}, u32[]{:S(2)}, u32[]{:S(2)}) collective-permute-start(bf16[512,512]{1,0:T(8,128)(2,1)S(1)} %copy-done), channel_id=1, source_target_pairs={{0,1},{1,0},{2,3},{3,2},{4,5},{5,4},{6,7},{7,6},{8,9},{9,8},{10,11... | collective-permute-start | bytes 1572872 | tf_op jit(solution)/shard_map/ppermute | solution.py:242
  49.5 0.0 collective-permute-done.7.refs_5_.refs_7_
  49.5 0.2 collective-permute-start.11
  49.7 10.2 %collective-permute-done.9 = bf16[512,512]{1,0:T(8,128)(2,1)} collective-permute-done((bf16[512,512]{1,0:T(8,128)(2,1)}, bf16[512,512]{1,0:T(8,128)(2,1)}, u32[]{:S(2)}, u32[]{:S(2)}) %collective-permute-start.9) | collective-permute-done | bytes 524320 | tf_op jit(solution)/shard_map/ppermute | solution.py:242
  59.9 2.1 %collective-permute-start.8 = (bf16[512,512]{1,0:T(8,128)(2,1)}, bf16[512,512]{1,0:T(8,128)(2,1)}, u32[]{:S(2)}, u32[]{:S(2)}) collective-permute-start(bf16[512,512]{1,0:T(8,128)(2,1)} %collective-permute-done.7.refs_5_.refs_7_), channel_id=1, source_target_pairs={{0,2},{1,7},{2,4},{3,1},{4,6},{5,3},{6,0},{7,5},{8,10},{9,15},{10,... | collective-permute-start | bytes 1572872 | tf_op jit(solution)/shard_map/ppermute | solution.py:242
  61.9 0.0 collective-permute-done.6.refs_9_.refs_8_
  61.9 1.6 %collective-permute-start.10 = (bf16[512,512]{1,0:T(8,128)(2,1)}, bf16[512,512]{1,0:T(8,128)(2,1)}, u32[]{:S(2)}, u32[]{:S(2)}) collective-permute-start(bf16[512,512]{1,0:T(8,128)(2,1)} %collective-permute-done.9), channel_id=1, source_target_pairs={{0,2},{1,7},{2,4},{3,1},{4,6},{5,3},{6,0},{7,5},{8,10},{9,15},{10,... | collective-permute-start | bytes 1572872 | tf_op jit(solution)/shard_map/ppermute | solution.py:242
  63.6 5.0 %shard_map.52.refs_4_ = bf16[512,512]{1,0:T(8,128)(2,1)} custom-call(bf16[512,512]{1,0:T(8,128)(2,1)} %get-tuple-element.33.refs_0_, bf16[512,512]{1,0:T(8,128)(2,1)} %get-tuple-element.30.refs_1_.refs_7_.refs_0_, bf16[512,512]{1,0:T(8,128)(2,1)} %get-tuple-element.35.refs_2_, bf16[512,512]{1,0:T(8,128)(2,1)} %copy-done.3, ...), custom_call_target="tpu_custom_call" | custom-call | tf_op jit(solution)/shard_map/pallas_call | solution.py:214
  68.6 0.0 collective-permute-done.13.refs_6_
  68.6 2.7 %collective-permute-start.17 = (bf16[512,512]{1,0:T(8,128)(2,1)}, bf16[512,512]{1,0:T(8,128)(2,1)}, u32[]{:S(2)}, u32[]{:S(2)}) collective-permute-start(bf16[512,512]{1,0:T(8,128)(2,1)} %shard_map.52.refs_4_), channel_id=1, source_target_pairs={{0,1},{1,0},{2,3},{3,2},{4,5},{5,4},{6,7},{7,6},{8,9},{9,8},{10,11... | collective-permute-start | bytes 1572872 | tf_op jit(solution)/shard_map/ppermute | solution.py:242
  71.3 0.0 collective-permute-done.refs_3_
  71.3 1.9 %collective-permute-start.1 = (bf16[512,512]{1,0:T(8,128)(2,1)}, bf16[512,512]{1,0:T(8,128)(2,1)S(1)}, u32[]{:S(2)}, u32[]{:S(2)}) collective-permute-start(bf16[512,512]{1,0:T(8,128)(2,1)} %collective-permute-done.refs_3_), channel_id=1, source_target_pairs={{0,2},{1,7},{2,4},{3,1},{4,6},{5,3},{6,0},{7,5},{8,10},{9,15},{10,... | collective-permute-start | bytes 1572872 | tf_op jit(solution)/shard_map/ppermute | solution.py:242
  73.2 0.0 collective-permute-done.11.refs_3_
  73.2 0.0 collective-permute-start.20
  73.2 3.9 %collective-permute-done.8.refs_5_ = bf16[512,512]{1,0:T(8,128)(2,1)} collective-permute-done((bf16[512,512]{1,0:T(8,128)(2,1)}, bf16[512,512]{1,0:T(8,128)(2,1)}, u32[]{:S(2)}, u32[]{:S(2)}) %collective-permute-start.8) | collective-permute-done | bytes 524320 | tf_op jit(solution)/shard_map/ppermute | solution.py:242
  77.1 0.0 collective-permute-start.21
  77.1 11.2 %collective-permute-done.10.refs_6_ = bf16[512,512]{1,0:T(8,128)(2,1)} collective-permute-done((bf16[512,512]{1,0:T(8,128)(2,1)}, bf16[512,512]{1,0:T(8,128)(2,1)}, u32[]{:S(2)}, u32[]{:S(2)}) %collective-permute-start.10) | collective-permute-done | bytes 524320 | tf_op jit(solution)/shard_map/ppermute | solution.py:242
  88.3 0.0 copy-done.5
  88.3 1.0 collective-permute-start.19
  89.3 0.0 collective-permute-done.17.refs_3_
  89.3 0.5 collective-permute-start.18
  89.8 7.4 %shard_map.53 = (bf16[4,16,128,128]{3,2,1,0:T(8,128)(2,1)}, bf16[512,512]{1,0:T(8,128)(2,1)}, f32[512,512]{1,0:T(8,128)}, f32[512,512]{1,0:T(8,128)}) custom-call(bf16[512,512]{1,0:T(8,128)(2,1)} %get-tuple-element.33.refs_0_, bf16[512,512]{1,0:T(8,128)(2,1)} %get-tuple-element.38.refs_1_.refs_2_, bf16[512,512]{1,0:T(8,128)(2,1)} %get-tuple-element.35.refs_2_, ...), custom_call_target="tpu_custom_call" | custom-call | tf_op jit(solution)/shard_map/pallas_call | solution.py:214
  97.2 7.2 %shard_map.54 = (bf16[4,16,128,128]{3,2,1,0:T(8,128)(2,1)}, bf16[512,512]{1,0:T(8,128)(2,1)}, f32[512,512]{1,0:T(8,128)}, f32[512,512]{1,0:T(8,128)}) custom-call(bf16[512,512]{1,0:T(8,128)(2,1)} %get-tuple-element.33.refs_0_, bf16[512,512]{1,0:T(8,128)(2,1)} %get-tuple-element.36.refs_1_.refs_5_, ...), custom_call_target="tpu_custom_call", output_to_operand_aliasing={{0}: (13, {})} | custom-call | tf_op jit(solution)/shard_map/pallas_call | solution.py:214
  104.4 5.5 %shard_map.55 = (bf16[4,16,128,128]{3,2,1,0:T(8,128)(2,1)}, bf16[512,512]{1,0:T(8,128)(2,1)}) custom-call(bf16[512,512]{1,0:T(8,128)(2,1)} %get-tuple-element.33.refs_0_, bf16[512,512]{1,0:T(8,128)(2,1)} %get-tuple-element.40.refs_1_.refs_2_.refs_9_, bf16[512,512]{1,0:T(8,128)(2,1)} %get-tuple-element.52.refs_6_.refs_2_, ...), custom_call_target="tpu_custom_call", output_to_operand_aliasing={{0}: (8, {})} | custom-call | tf_op jit(solution)/shard_map/pallas_call | solution.py:214
  109.9 0.0 collective-permute-done.1.refs_3_
  109.9 0.0 copy-start.14
  109.9 0.8 copy-done.14
  110.7 7.2 %shard_map.56 = (bf16[4,16,128,128]{3,2,1,0:T(8,128)(2,1)}, bf16[512,512]{1,0:T(8,128)(2,1)}, f32[512,512]{1,0:T(8,128)}, f32[512,512]{1,0:T(8,128)}) custom-call(bf16[512,512]{1,0:T(8,128)(2,1)} %get-tuple-element.33.refs_0_, bf16[512,512]{1,0:T(8,128)(2,1)} %get-tuple-element.31.refs_1_.refs_2_, ...), custom_call_target="tpu_custom_call", output_to_operand_aliasing={{0}: (13, {})} | custom-call | tf_op jit(solution)/shard_map/pallas_call | solution.py:214
  117.9 0.0 collective-permute-done.20.refs_3_
  117.9 0.0 copy-start.12
  117.9 0.0 collective-permute-done.21.refs_6_
  117.9 0.8 copy-done.12
  118.7 0.1 copy-done.13
  118.9 4.8 %shard_map.57.refs_6_ = bf16[4,16,128,128]{3,2,1,0:T(8,128)(2,1)} custom-call(bf16[512,512]{1,0:T(8,128)(2,1)} %get-tuple-element.30.refs_1_.refs_7_.refs_0_, bf16[512,512]{1,0:T(8,128)(2,1)} %get-tuple-element.55.refs_1_, bf16[512,512]{1,0:T(8,128)(2,1)} %get-tuple-element.38.refs_1_.refs_2_, bf16[512,512]{1,0:T(8,128)(2,1)} %copy-done.12, ...), custom_call_target="tpu_custom_call" | custom-call | tf_op jit(solution)/shard_map/pallas_call | solution.py:214
  123.7 3.8 %shard_map.58.refs_13_ = bf16[4,16,128,128]{3,2,1,0:T(8,128)(2,1)} custom-call(bf16[512,512]{1,0:T(8,128)(2,1)} %get-tuple-element.30.refs_1_.refs_7_.refs_0_, bf16[512,512]{1,0:T(8,128)(2,1)} %get-tuple-element.51.refs_1_.refs_4_, bf16[512,512]{1,0:T(8,128)(2,1)} %get-tuple-element.40.refs_1_.refs_2_.refs_9_, ...), custom_call_target="tpu_custom_call", output_to_operand_aliasing={{}: (6, {})} | custom-call | tf_op jit(solution)/shard_map/pallas_call | solution.py:214
  127.5 0.0 collective-permute-done.19.refs_5_
  127.5 0.0 copy-start.10
  127.5 0.0 collective-permute-done.18.refs_3_
  127.5 0.8 copy-done.10
  128.3 0.2 copy-done.11
  128.5 6.0 %shard_map.59 = (bf16[4,16,128,128]{3,2,1,0:T(8,128)(2,1)}, bf16[4,16,128,128]{3,2,1,0:T(8,128)(2,1)}) custom-call(bf16[512,512]{1,0:T(8,128)(2,1)} %get-tuple-element.30.refs_1_.refs_7_.refs_0_, bf16[512,512]{1,0:T(8,128)(2,1)} %get-tuple-element.50.refs_1_, ...), custom_call_target="tpu_custom_call", output_to_operand_aliasing={{0}: (13, {}), {1}: (14, {})} | custom-call | tf_op jit(solution)/shard_map/pallas_call | solution.py:214
  (21 shorter events, 0.0 us)
Async XLA Ops:
  7.1 26.4 %copy-start = (bf16[512,512]{1,0:T(8,128)(2,1)S(1)}, bf16[512,512]{1,0:T(8,128)(2,1)}, u32[]{:S(2)}) copy-start(bf16[512,512]{1,0:T(8,128)(2,1)} %get-tuple-element.30.refs_1_.refs_7_.refs_0_) | copy-start | bytes 1572868
  7.1 16.0 %collective-permute-start.5 = (bf16[512,512]{1,0:T(8,128)(2,1)}, bf16[512,512]{1,0:T(8,128)(2,1)S(1)}, u32[]{:S(2)}, u32[]{:S(2)}) collective-permute-start(bf16[512,512]{1,0:T(8,128)(2,1)} %get-tuple-element.31.refs_1_.refs_2_), channel_id=1, source_target_pairs={{0,1},{1,0},{2,3},{3,2},{4,5},{5,4},{6,7},{7,6},{8,9},{9,8},{10,11... | collective-permute-start | bytes 1572872 | tf_op jit(solution)/shard_map/ppermute | solution.py:242
  10.1 23.4 %collective-permute-start.4 = (bf16[512,512]{1,0:T(8,128)(2,1)}, bf16[512,512]{1,0:T(8,128)(2,1)S(1)}, u32[]{:S(2)}, u32[]{:S(2)}) collective-permute-start(bf16[512,512]{1,0:T(8,128)(2,1)} %get-tuple-element.40.refs_1_.refs_2_.refs_9_), channel_id=1, source_target_pairs={{0,1},{1,0},{2,3},{3,2},{4,5},{5,4},{6,7},{7,6},{8,9},{9,8},{10,11... | collective-permute-start | bytes 1572872 | tf_op jit(solution)/shard_map/ppermute | solution.py:242
  10.2 23.7 %collective-permute-start.2 = (bf16[512,512]{1,0:T(8,128)(2,1)}, bf16[512,512]{1,0:T(8,128)(2,1)S(1)}, u32[]{:S(2)}, u32[]{:S(2)}) collective-permute-start(bf16[512,512]{1,0:T(8,128)(2,1)} %get-tuple-element.36.refs_1_.refs_5_), channel_id=1, source_target_pairs={{0,24},{8,0},{16,8},{24,16},{1,25},{9,1},{17,9},{25,17},{2,26},{10... | collective-permute-start | bytes 1572872 | tf_op jit(solution)/shard_map/ppermute | solution.py:242
  11.0 23.0 %collective-permute-start.3 = (bf16[512,512]{1,0:T(8,128)(2,1)}, bf16[512,512]{1,0:T(8,128)(2,1)S(1)}, u32[]{:S(2)}, u32[]{:S(2)}) collective-permute-start(bf16[512,512]{1,0:T(8,128)(2,1)} %get-tuple-element.38.refs_1_.refs_2_), channel_id=1, source_target_pairs={{0,8},{8,16},{16,24},{24,0},{1,9},{9,17},{17,25},{25,1},{2,10},{10... | collective-permute-start | bytes 1572872 | tf_op jit(solution)/shard_map/ppermute | solution.py:242
  17.0 18.7 %collective-permute-start.15 = (bf16[512,512]{1,0:T(8,128)(2,1)}, bf16[512,512]{1,0:T(8,128)(2,1)S(1)}, u32[]{:S(2)}, u32[]{:S(2)}) collective-permute-start(bf16[512,512]{1,0:T(8,128)(2,1)} %get-tuple-element.33.refs_0_), channel_id=1, source_target_pairs={{0,24},{8,0},{16,8},{24,16},{1,25},{9,1},{17,9},{25,17},{2,26},{10... | collective-permute-start | bytes 1572872 | tf_op jit(solution)/shard_map/ppermute | solution.py:242
  23.1 12.9 %collective-permute-start.16 = (bf16[512,512]{1,0:T(8,128)(2,1)}, bf16[512,512]{1,0:T(8,128)(2,1)S(1)}, u32[]{:S(2)}, u32[]{:S(2)}) collective-permute-start(bf16[512,512]{1,0:T(8,128)(2,1)} %get-tuple-element.37.refs_4_.refs_2_), channel_id=1, source_target_pairs={{0,24},{8,0},{16,8},{24,16},{1,25},{9,1},{17,9},{25,17},{2,26},{10... | collective-permute-start | bytes 1572872 | tf_op jit(solution)/shard_map/ppermute | solution.py:242
  33.5 30.1 %copy-start.1 = (bf16[512,512]{1,0:T(8,128)(2,1)}, bf16[512,512]{1,0:T(8,128)(2,1)S(1)}, u32[]{:S(2)}) copy-start(bf16[512,512]{1,0:T(8,128)(2,1)S(1)} %collective-permute-done.4.refs_7_.refs_8_) | copy-start | bytes 1572868
  33.5 11.5 %collective-permute-start.14 = (bf16[512,512]{1,0:T(8,128)(2,1)S(1)}, bf16[512,512]{1,0:T(8,128)(2,1)S(1)}, u32[]{:S(2)}, u32[]{:S(2)}) collective-permute-start(bf16[512,512]{1,0:T(8,128)(2,1)S(1)} %copy-done), channel_id=1, source_target_pairs={{0,24},{8,0},{16,8},{24,16},{1,25},{9,1},{17,9},{25,17},{2,26},{10... | collective-permute-start | bytes 1572872 | tf_op jit(solution)/shard_map/ppermute | solution.py:242
  33.8 29.7 %copy-start.3 = (bf16[512,512]{1,0:T(8,128)(2,1)}, bf16[512,512]{1,0:T(8,128)(2,1)S(1)}, u32[]{:S(2)}) copy-start(bf16[512,512]{1,0:T(8,128)(2,1)S(1)} %collective-permute-done.2.refs_3_.refs_8_) | copy-start | bytes 1572868
  33.8 14.2 %collective-permute-start.12 = (bf16[512,512]{1,0:T(8,128)(2,1)}, bf16[512,512]{1,0:T(8,128)(2,1)S(1)}, u32[]{:S(2)}, u32[]{:S(2)}) collective-permute-start(bf16[512,512]{1,0:T(8,128)(2,1)} %get-tuple-element.33.refs_0_), channel_id=1, source_target_pairs={{0,8},{8,16},{16,24},{24,0},{1,9},{9,17},{17,25},{25,1},{2,10},{10... | collective-permute-start | bytes 1572872 | tf_op jit(solution)/shard_map/ppermute | solution.py:242
  34.0 29.6 %copy-start.2 = (bf16[512,512]{1,0:T(8,128)(2,1)}, bf16[512,512]{1,0:T(8,128)(2,1)S(1)}, u32[]{:S(2)}) copy-start(bf16[512,512]{1,0:T(8,128)(2,1)S(1)} %collective-permute-done.3.refs_5_.refs_8_) | copy-start | bytes 1572868
  34.0 15.5 %collective-permute-start.7 = (bf16[512,512]{1,0:T(8,128)(2,1)}, bf16[512,512]{1,0:T(8,128)(2,1)}, u32[]{:S(2)}, u32[]{:S(2)}) collective-permute-start(bf16[512,512]{1,0:T(8,128)(2,1)} %get-tuple-element.33.refs_0_), channel_id=1, source_target_pairs={{0,1},{1,0},{2,3},{3,2},{4,5},{5,4},{6,7},{7,6},{8,9},{9,8},{10,11... | collective-permute-start | bytes 1572872 | tf_op jit(solution)/shard_map/ppermute | solution.py:242
  35.7 27.8 %copy-start.6 = (bf16[512,512]{1,0:T(8,128)(2,1)}, bf16[512,512]{1,0:T(8,128)(2,1)S(1)}, u32[]{:S(2)}) copy-start(bf16[512,512]{1,0:T(8,128)(2,1)S(1)} %collective-permute-done.15.refs_5_) | copy-start | bytes 1572868
  35.7 24.1 %collective-permute-start.9 = (bf16[512,512]{1,0:T(8,128)(2,1)}, bf16[512,512]{1,0:T(8,128)(2,1)}, u32[]{:S(2)}, u32[]{:S(2)}) collective-permute-start(bf16[512,512]{1,0:T(8,128)(2,1)} %get-tuple-element.34.refs_8_.refs_2_), channel_id=1, source_target_pairs={{0,1},{1,0},{2,3},{3,2},{4,5},{5,4},{6,7},{7,6},{8,9},{9,8},{10,11... | collective-permute-start | bytes 1572872 | tf_op jit(solution)/shard_map/ppermute | solution.py:242
  36.0 27.5 %copy-start.7 = (bf16[512,512]{1,0:T(8,128)(2,1)}, bf16[512,512]{1,0:T(8,128)(2,1)S(1)}, u32[]{:S(2)}) copy-start(bf16[512,512]{1,0:T(8,128)(2,1)S(1)} %collective-permute-done.16.refs_6_) | copy-start | bytes 1572868
  36.0 25.9 %collective-permute-start.6 = (bf16[512,512]{1,0:T(8,128)(2,1)S(1)}, bf16[512,512]{1,0:T(8,128)(2,1)S(1)}, u32[]{:S(2)}, u32[]{:S(2)}) collective-permute-start(bf16[512,512]{1,0:T(8,128)(2,1)S(1)} %collective-permute-done.5), channel_id=1, source_target_pairs={{0,2},{1,7},{2,4},{3,1},{4,6},{5,3},{6,0},{7,5},{8,10},{9,15},{10,... | collective-permute-start | bytes 1572872 | tf_op jit(solution)/shard_map/ppermute | solution.py:242
  45.0 18.5 %copy-start.9 = (bf16[512,512]{1,0:T(8,128)(2,1)}, bf16[512,512]{1,0:T(8,128)(2,1)S(1)}, u32[]{:S(2)}) copy-start(bf16[512,512]{1,0:T(8,128)(2,1)S(1)} %collective-permute-done.14.refs_3_) | copy-start | bytes 1572868
  45.0 23.6 %collective-permute-start.13 = (bf16[512,512]{1,0:T(8,128)(2,1)}, bf16[512,512]{1,0:T(8,128)(2,1)}, u32[]{:S(2)}, u32[]{:S(2)}) collective-permute-start(bf16[512,512]{1,0:T(8,128)(2,1)} %get-tuple-element.35.refs_2_), channel_id=1, source_target_pairs={{0,8},{8,16},{16,24},{24,0},{1,9},{9,17},{17,25},{25,1},{2,10},{10... | collective-permute-start | bytes 1572872 | tf_op jit(solution)/shard_map/ppermute | solution.py:242
  48.0 15.5 %copy-start.8 = (bf16[512,512]{1,0:T(8,128)(2,1)}, bf16[512,512]{1,0:T(8,128)(2,1)S(1)}, u32[]{:S(2)}) copy-start(bf16[512,512]{1,0:T(8,128)(2,1)S(1)} %collective-permute-done.12.refs_5_) | copy-start | bytes 1572868
  48.0 23.3 %collective-permute-start = (bf16[512,512]{1,0:T(8,128)(2,1)S(1)}, bf16[512,512]{1,0:T(8,128)(2,1)}, u32[]{:S(2)}, u32[]{:S(2)}) collective-permute-start(bf16[512,512]{1,0:T(8,128)(2,1)S(1)} %copy-done), channel_id=1, source_target_pairs={{0,1},{1,0},{2,3},{3,2},{4,5},{5,4},{6,7},{7,6},{8,9},{9,8},{10,11... | collective-permute-start | bytes 1572872 | tf_op jit(solution)/shard_map/ppermute | solution.py:242
  49.5 23.7 %collective-permute-start.11 = (bf16[512,512]{1,0:T(8,128)(2,1)S(1)}, bf16[512,512]{1,0:T(8,128)(2,1)}, u32[]{:S(2)}, u32[]{:S(2)}) collective-permute-start(bf16[512,512]{1,0:T(8,128)(2,1)S(1)} %copy-done), channel_id=1, source_target_pairs={{0,8},{8,16},{16,24},{24,0},{1,9},{9,17},{17,25},{25,1},{2,10},{10... | collective-permute-start | bytes 1572872 | tf_op jit(solution)/shard_map/ppermute | solution.py:242
  59.9 17.2 %collective-permute-start.8 = (bf16[512,512]{1,0:T(8,128)(2,1)}, bf16[512,512]{1,0:T(8,128)(2,1)}, u32[]{:S(2)}, u32[]{:S(2)}) collective-permute-start(bf16[512,512]{1,0:T(8,128)(2,1)} %collective-permute-done.7.refs_5_.refs_7_), channel_id=1, source_target_pairs={{0,2},{1,7},{2,4},{3,1},{4,6},{5,3},{6,0},{7,5},{8,10},{9,15},{10,... | collective-permute-start | bytes 1572872 | tf_op jit(solution)/shard_map/ppermute | solution.py:242
  61.9 1.6 %copy-start.4 = (bf16[512,512]{1,0:T(8,128)(2,1)}, bf16[512,512]{1,0:T(8,128)(2,1)S(1)}, u32[]{:S(2)}) copy-start(bf16[512,512]{1,0:T(8,128)(2,1)S(1)} %collective-permute-done.6.refs_9_.refs_8_) | copy-start | bytes 1572868
  61.9 26.3 %collective-permute-start.10 = (bf16[512,512]{1,0:T(8,128)(2,1)}, bf16[512,512]{1,0:T(8,128)(2,1)}, u32[]{:S(2)}, u32[]{:S(2)}) collective-permute-start(bf16[512,512]{1,0:T(8,128)(2,1)} %collective-permute-done.9), channel_id=1, source_target_pairs={{0,2},{1,7},{2,4},{3,1},{4,6},{5,3},{6,0},{7,5},{8,10},{9,15},{10,... | collective-permute-start | bytes 1572872 | tf_op jit(solution)/shard_map/ppermute | solution.py:242
  63.6 24.7 %copy-start.5 = (bf16[512,512]{1,0:T(8,128)(2,1)S(1)}, bf16[512,512]{1,0:T(8,128)(2,1)}, u32[]{:S(2)}) copy-start(bf16[512,512]{1,0:T(8,128)(2,1)} %get-tuple-element.52.refs_6_.refs_2_) | copy-start | bytes 1572868
  68.6 20.7 %collective-permute-start.17 = (bf16[512,512]{1,0:T(8,128)(2,1)}, bf16[512,512]{1,0:T(8,128)(2,1)}, u32[]{:S(2)}, u32[]{:S(2)}) collective-permute-start(bf16[512,512]{1,0:T(8,128)(2,1)} %shard_map.52.refs_4_), channel_id=1, source_target_pairs={{0,1},{1,0},{2,3},{3,2},{4,5},{5,4},{6,7},{7,6},{8,9},{9,8},{10,11... | collective-permute-start | bytes 1572872 | tf_op jit(solution)/shard_map/ppermute | solution.py:242
  71.3 38.6 %collective-permute-start.1 = (bf16[512,512]{1,0:T(8,128)(2,1)}, bf16[512,512]{1,0:T(8,128)(2,1)S(1)}, u32[]{:S(2)}, u32[]{:S(2)}) collective-permute-start(bf16[512,512]{1,0:T(8,128)(2,1)} %collective-permute-done.refs_3_), channel_id=1, source_target_pairs={{0,2},{1,7},{2,4},{3,1},{4,6},{5,3},{6,0},{7,5},{8,10},{9,15},{10,... | collective-permute-start | bytes 1572872 | tf_op jit(solution)/shard_map/ppermute | solution.py:242
  73.2 44.7 %collective-permute-start.20 = (bf16[512,512]{1,0:T(8,128)(2,1)}, bf16[512,512]{1,0:T(8,128)(2,1)S(1)}, u32[]{:S(2)}, u32[]{:S(2)}) collective-permute-start(bf16[512,512]{1,0:T(8,128)(2,1)} %shard_map.52.refs_4_), channel_id=1, source_target_pairs={{0,24},{8,0},{16,8},{24,16},{1,25},{9,1},{17,9},{25,17},{2,26},{10... | collective-permute-start | bytes 1572872 | tf_op jit(solution)/shard_map/ppermute | solution.py:242
  77.1 40.9 %collective-permute-start.21 = (bf16[512,512]{1,0:T(8,128)(2,1)}, bf16[512,512]{1,0:T(8,128)(2,1)S(1)}, u32[]{:S(2)}, u32[]{:S(2)}) collective-permute-start(bf16[512,512]{1,0:T(8,128)(2,1)} %shard_map.52.refs_4_), channel_id=1, source_target_pairs={{0,8},{8,16},{16,24},{24,0},{1,9},{9,17},{17,25},{25,1},{2,10},{10... | collective-permute-start | bytes 1572872 | tf_op jit(solution)/shard_map/ppermute | solution.py:242
  88.3 39.2 %collective-permute-start.19 = (bf16[512,512]{1,0:T(8,128)(2,1)S(1)}, bf16[512,512]{1,0:T(8,128)(2,1)S(1)}, u32[]{:S(2)}, u32[]{:S(2)}) collective-permute-start(bf16[512,512]{1,0:T(8,128)(2,1)S(1)} %copy-done.5), channel_id=1, source_target_pairs={{0,1},{1,0},{2,3},{3,2},{4,5},{5,4},{6,7},{7,6},{8,9},{9,8},{10,11... | collective-permute-start | bytes 1572872 | tf_op jit(solution)/shard_map/ppermute | solution.py:242
  89.3 38.2 %collective-permute-start.18 = (bf16[512,512]{1,0:T(8,128)(2,1)}, bf16[512,512]{1,0:T(8,128)(2,1)S(1)}, u32[]{:S(2)}, u32[]{:S(2)}) collective-permute-start(bf16[512,512]{1,0:T(8,128)(2,1)} %collective-permute-done.17.refs_3_), channel_id=1, source_target_pairs={{0,2},{1,7},{2,4},{3,1},{4,6},{5,3},{6,0},{7,5},{8,10},{9,15},{10,... | collective-permute-start | bytes 1572872 | tf_op jit(solution)/shard_map/ppermute | solution.py:242
  109.9 0.8 copy-start.14
  117.9 0.8 copy-start.12
  117.9 0.9 copy-start.13
  127.5 0.8 copy-start.10
  127.5 1.0 copy-start.11

commit v2 on v1

v2 whole, which is shorter than its diff:
```python
import functools

import jax
import jax.numpy as jnp
from jax import lax
from jax.experimental import pallas as pl
from jax.experimental.pallas import tpu as pltpu
from jax.sharding import PartitionSpec as P


HBM = pl.BlockSpec(memory_space=pltpu.HBM)
SMEM = pl.BlockSpec(memory_space=pltpu.SMEM)
VMEM = pl.BlockSpec(memory_space=pltpu.VMEM)
GRANT = 24 << 20

OWN, PARTNER, BEYOND, UPPER, LOWER = range(5)


def slot_domains(row_count, col_count):
    coord_x = lax.axis_index("row")
    coord_y = lax.axis_index("col")
    step = 1 - 2 * lax.rem(coord_y, 2)
    partner = coord_y + step
    beyond = lax.rem(coord_y - step + col_count, col_count)
    upper = lax.rem(coord_x + 1, row_count)
    lower = lax.rem(coord_x + row_count - 1, row_count)
    return (
        coord_x * col_count + coord_y,
        coord_x * col_count + partner,
        coord_x * col_count + beyond,
        upper * col_count + coord_y,
        lower * col_count + coord_y,
    )


def split(column, rows):
    if rows & (rows - 1) == 0:
        return lax.shift_right_logical(column, rows.bit_length() - 1), column & (rows - 1)
    domain = lax.div(column, rows)
    return domain, column - domain * rows


def copy_slots(slots, rows, table, blocks, units, in_sem):
    size = blocks.shape[2]
    todo = []
    for i, slot in enumerate(slots):
        for z in range(rows):
            for depth in range(rows):
                place = table[(z * 5 + slot) * rows + depth]
                where = units[i].at[pl.ds(z * size, size), pl.ds(depth * size, size)]
                copy = pltpu.make_async_copy(
                    blocks.at[z, jnp.maximum(place, 0)], where, in_sem
                )

                @pl.when(place >= 0)
                def _(copy=copy):
                    copy.start()

                @pl.when(place < 0)
                def _(where=where):
                    where[...] = jnp.zeros(where.shape, where.dtype)

                todo.append((place, copy))
    return todo


def finish_slots(todo):
    for place, copy in todo:

        @pl.when(place >= 0)
        def _(copy=copy):
            copy.wait()


def first_pack_body(slots, grid, columns, blocks, *refs):
    rows, lanes = blocks.shape[:2]
    units, (table, in_sem) = refs[: len(slots)], refs[len(slots) :]
    domains = slot_domains(*grid)
    for i in range(rows * 5 * rows):
        table[i] = -1
    for z in range(rows):
        for k in range(lanes):
            domain, depth = split(columns[k, domains[0] * rows + z], rows)
            slot = jnp.int32(OWN)
            for other in range(1, 5):
                slot = jnp.where(domain == domains[other], other, slot)
            table[(z * 5 + slot) * rows + depth] = k
    finish_slots(copy_slots(slots, rows, table, blocks, units, in_sem))


def pack_body(slots, table, blocks, *refs):
    units, (in_sem,) = refs[: len(slots)], refs[len(slots) :]
    finish_slots(copy_slots(slots, blocks.shape[0], table, blocks, units, in_sem))


def near_pack_body(slots, grid, columns, table, blocks, *refs):
    rows, lanes = blocks.shape[:2]
    units, (near, top, bottom, in_sem) = refs[: len(slots)], refs[len(slots) :]
    todo = copy_slots(slots, rows, table, blocks, units, in_sem)
    domains = slot_domains(*grid)
    for i in range(5 * rows * rows):
        near[i] = 0

    @pl.loop(0, lanes)
    def _(k):
        for slot in range(1, 5):
            for z in range(rows):
                domain, depth = split(columns[k, domains[slot] * rows + z], rows)
                place = (slot * rows + z) * rows + depth
                near[place] = jnp.where(domain == domains[0], 1, near[place])

    finish_slots(todo)
    own, half = units[slots.index(OWN)], top.shape[0]
    top[...] = own[:half]
    bottom[...] = own[half:]


def half_of(blocks):
    order = blocks.shape[0] * blocks.shape[2]
    return jax.ShapeDtypeStruct((order // 2, order), blocks.dtype)


def pack(slots, blocks, columns=None, table=None, grid=None):
    rows, _, size, _ = blocks.shape
    order = rows * size
    entries = jax.ShapeDtypeStruct((5 * rows * rows,), jnp.int32)
    if table is None:
        body, operands = functools.partial(first_pack_body, slots, grid), (columns, blocks)
    elif columns is None:
        body, operands = functools.partial(pack_body, slots), (table, blocks)
    else:
        body, operands = functools.partial(near_pack_body, slots, grid), (columns, table, blocks)
    extra = [] if columns is None else [entries]
    halves = [] if columns is None or table is None else [half_of(blocks)] * 2
    return pl.pallas_call(
        body,
        out_shape=[jax.ShapeDtypeStruct((order, order), blocks.dtype)] * len(slots) + extra + halves,
        in_specs=[SMEM] * (len(operands) - 1) + [HBM],
        out_specs=[VMEM] * len(slots) + [SMEM] * len(extra) + [VMEM] * len(halves),
        scratch_shapes=[pltpu.SemaphoreType.DMA],
        compiler_params=pltpu.CompilerParams(vmem_limit_bytes=GRANT),
    )(*operands)


class Stage:
    def __init__(self, loads, table, near, sinks, outs, blocks_sem, size):
        self.loads, self.table, self.near = loads, table, near
        self.sinks, self.outs, self.blocks_sem, self.size = sinks, outs, blocks_sem, size
        self.pending = []

    def load(self, key):
        if key in self.loads:
            return self.loads[key][...]
        return jnp.concatenate([self.loads[key + "_top"][...], self.loads[key + "_low"][...]], axis=0)

    def dot(self, *pairs):
        value = lambda x: self.load(x) if isinstance(x, str) else x[...]
        lefts = [value(left) for left, _ in pairs]
        rights = [value(right) for _, right in pairs]
        left = lefts[0] if len(pairs) == 1 else jnp.concatenate(lefts, axis=1)
        right = rights[0] if len(pairs) == 1 else jnp.concatenate(rights, axis=0)
        return jnp.dot(left, right, preferred_element_type=jnp.float32)

    def scaled(self, value, present, diagonal=False):
        size = self.size
        rows = value.shape[0] // size
        bands = []
        for z in range(rows):
            band = []
            for depth in range(rows):
                block = value[z * size : (z + 1) * size, depth * size : (depth + 1) * size]
                block = block * jnp.where(present(z, depth), jnp.float32(-0.5), jnp.float32(0.0))
                if diagonal and z == depth:
                    r = lax.broadcasted_iota(jnp.int32, (size, size), 0)
                    c = lax.broadcasted_iota(jnp.int32, (size, size), 1)
                    block = block + jnp.where(r == c, jnp.float32(1.5), jnp.float32(0.0))
                band.append(block)
            bands.append(jnp.concatenate(band, axis=1))
        return jnp.concatenate(bands, axis=0).astype(jnp.bfloat16)

    def own_present(self, slot, rows):
        return lambda z, depth: self.table[(z * 5 + slot) * rows + depth] >= 0

    def near_present(self, slot, rows):
        return lambda z, depth: self.near[(slot * rows + z) * rows + depth] > 0

    def emit(self, sink, slot, staging, value):
        size = self.size
        rows = value.shape[0] // size
        staging[...] = value.astype(staging.dtype)
        target = self.sinks[sink]
        for z in range(rows):
            for depth in range(rows):
                place = self.table[(z * 5 + slot) * rows + depth]
                copy = pltpu.make_async_copy(
                    staging.at[pl.ds(z * size, size), pl.ds(depth * size, size)],
                    target.at[z, jnp.maximum(place, 0)],
                    self.blocks_sem.at[len(self.pending)],
                )

                @pl.when(place >= 0)
                def _(copy=copy):
                    copy.start()

                self.pending.append((place, copy))

    def finish(self):
        for place, copy in self.pending:

            @pl.when(place >= 0)
            def _(copy=copy):
                copy.wait()


def stage_call(body, loads, tables, sinks, outs, sparse_shape, emits):
    keys, sink_keys, out_keys = list(loads), list(sinks), list(outs)
    known = [key for key in sink_keys if sinks[key] is not None]
    size = sparse_shape.shape[2]
    order = sparse_shape.shape[0] * size

    def kernel(*refs):
        refs = list(refs)
        take = lambda n: [refs.pop(0) for _ in range(n)]
        sources = take(len(keys))
        table, near = take(2)
        take(len(known))
        targets = take(len(sink_keys))
        results = take(len(out_keys))
        stagings = take(emits)
        (blocks_sem,) = take(1)
        stage = Stage(
            dict(zip(keys, sources)),
            table,
            near,
            dict(zip(sink_keys, targets)),
            dict(zip(out_keys, results)),
            blocks_sem,
            size,
        )
        body(stage, stagings)
        stage.finish()

    first_sink = len(keys) + 2
    return pl.pallas_call(
        kernel,
        out_shape=[sparse_shape] * len(sink_keys) + [outs[key] for key in out_keys],
        in_specs=[VMEM] * len(keys) + [SMEM] * 2 + [HBM] * len(known),
        out_specs=[HBM] * len(sink_keys) + [VMEM] * len(out_keys),
        scratch_shapes=[pltpu.VMEM((order, order), sparse_shape.dtype)] * emits
        + [pltpu.SemaphoreType.DMA((max(1, emits * sparse_shape.shape[0] ** 2),))],
        compiler_params=pltpu.CompilerParams(vmem_limit_bytes=GRANT),
        input_output_aliases={
            first_sink + i: sink_keys.index(key) for i, key in enumerate(known)
        },
    )(*[loads[key] for key in keys], *tables, *[sinks[key] for key in known])


def on_device(y_blocks, z_blocks, pattern):
    row_count, col_count = lax.axis_size("row"), lax.axis_size("col")
    rows, _, size, _ = y_blocks.shape
    order = rows * size
    grid = (row_count, col_count)
    swap = [(i, i ^ 1) for i in range(col_count)]
    hop = [(i, (i + 2 - 4 * (i % 2)) % col_count) for i in range(col_count)]
    upward = [(i, (i + 1) % row_count) for i in range(row_count)]
    downward = [(i, (i - 1) % row_count) for i in range(row_count)]

    def move(axis, route, value):
        return lax.ppermute(value, axis, route)

    sparse = jax.ShapeDtypeStruct(y_blocks.shape, y_blocks.dtype)
    unit = jax.ShapeDtypeStruct((order, order), y_blocks.dtype)
    sums = jax.ShapeDtypeStruct((order, order), jnp.float32)

    columns = pattern.T
    y_blocks = pltpu.with_memory_space_constraint(y_blocks, pltpu.HBM)
    z_blocks = pltpu.with_memory_space_constraint(z_blocks, pltpu.HBM)
    columns = pltpu.with_memory_space_constraint(columns, pltpu.HBM)
    yb, table = pack((BEYOND,), y_blocks, columns=columns, grid=grid)
    yo, yp, ym, ya = pack((OWN, UPPER, LOWER, PARTNER), y_blocks, table=table)
    zb, zo, zp, zm, za, near, zo_top, zo_low = pack(
        (BEYOND, OWN, UPPER, LOWER, PARTNER), z_blocks, columns=columns, table=table, grid=grid
    )
    yb_seen = move("col", swap, yb)
    y_aa = move("col", swap, yo)
    zb_seen = move("col", swap, zb)
    y_ao = move("col", swap, ya)
    z_aa = [move("col", swap, zo_top), move("col", swap, zo_low)]
    y_po, y_mo = move("row", downward, ym), move("row", upward, yp)
    y_pp, y_mm = move("row", downward, yo), move("row", upward, yo)
    z_pp, z_mm = move("row", downward, zo), move("row", upward, zo)
    z_po, z_mo = move("row", downward, zm), move("row", upward, zp)
    y_bo = move("col", hop, yb_seen)
    y_bb = move("col", hop, y_aa)
    z_bo = move("col", hop, zb_seen)
    z_bb = [move("col", hop, z_aa[0]), move("col", hop, z_aa[1])]

    def call(body, loads, sinks, outs, emits):
        loads = dict(loads)
        for key in [key for key in loads if isinstance(loads[key], list)]:
            loads[key + "_top"], loads[key + "_low"] = loads.pop(key)
        return stage_call(body, loads, (table, near), sinks, outs, sparse, emits)

    def outer_body(s, stagings):
        for i, slot in (("p", UPPER), ("m", LOWER), ("a", PARTNER), ("b", BEYOND)):
            value = s.dot(("zo", f"y{i}"), (f"z{i}", f"y_{i}{i}"))
            s.outs[f"t_o{i}"][...] = s.scaled(value, s.own_present(slot, rows))

    t_op, t_om, t_oa, t_ob = call(
        outer_body,
        dict(zo=zo, yp=yp, zp=zp, y_pp=y_pp, ym=ym, zm=zm, y_mm=y_mm, ya=ya, za=za, y_aa=y_aa, yb=yb, zb=zb, y_bb=y_bb),
        {}, dict(t_op=unit, t_om=unit, t_oa=unit, t_ob=unit), 0,
    )

    def own_body(s, stagings):
        value = s.dot(("zo", "yo"), ("zp", "y_po"), ("zm", "y_mo"), ("za", "y_ao"), ("zb", "y_bo"))
        value = s.scaled(value, s.own_present(OWN, rows), True)
        s.outs["t"][...] = value
        s.outs["t_top"][...] = value[: order // 2]
        s.outs["t_low"][...] = value[order // 2 :]

    half = half_of(y_blocks)
    to, to_top, to_low = call(
        own_body,
        dict(zo=zo, yo=yo, zp=zp, y_po=y_po, zm=zm, y_mo=y_mo, za=za, y_ao=y_ao, zb=zb, y_bo=y_bo),
        {}, dict(t=unit, t_top=half, t_low=half), 0,
    )
    t_aa = [move("col", swap, to_top), move("col", swap, to_low)]
    z_ao = move("col", swap, za)
    t_pp, t_mm = move("row", downward, to), move("row", upward, to)
    t_bb = [move("col", hop, t_aa[0]), move("col", hop, t_aa[1])]

    def rows_in_body(s, stagings):
        for i, slot, staging in (("p", UPPER, stagings[0]), ("m", LOWER, stagings[1])):
            value = s.dot((f"z_{i}o", "yo"), (f"z_{i}{i}", f"y_{i}o"))
            staging[...] = s.scaled(value, s.near_present(slot, rows))
        s.outs["y_sum"][...] = s.dot(("yo", "to"), ("yp", stagings[0]), ("ym", stagings[1]))
        s.outs["z_sum"][...] = s.dot(("to", "zo"), ("t_op", "z_po"), ("t_om", "z_mo"))

    y_sum, z_sum = call(
        rows_in_body,
        dict(z_po=z_po, yo=yo, z_pp=z_pp, y_po=y_po, z_mo=z_mo, z_mm=z_mm, y_mo=y_mo, to=to,
             yp=yp, ym=ym, zo=zo, t_op=t_op, t_om=t_om),
        {}, dict(y_sum=sums, z_sum=sums), 2,
    )

    def partner_body(s, stagings):
        s.emit("z", PARTNER, stagings[0], s.dot(("to", "za"), ("t_oa", "z_aa")))
        s.outs["a_sum"][...] = s.dot(("z_aa", "y_ao"))
        s.outs["b_sum"][...] = s.dot(("yo", "t_ob"))

    z_next, a_sum, b_sum = call(
        partner_body,
        dict(to=to, za=za, t_oa=t_oa, z_aa=z_aa, y_ao=y_ao, yo=yo, t_ob=t_ob),
        dict(z=None), dict(a_sum=sums, b_sum=sums), 1,
    )

    def rows_y_body(s, stagings):
        s.emit("y", UPPER, stagings[0], s.dot(("yo", "t_op"), ("yp", "t_pp")))
        s.emit("y", LOWER, stagings[1], s.dot(("yo", "t_om"), ("ym", "t_mm")))

    (y_next,) = call(
        rows_y_body,
        dict(yo=yo, t_op=t_op, yp=yp, t_pp=t_pp, t_om=t_om, ym=ym, t_mm=t_mm), dict(y=None), {}, 2,
    )

    def beyond_body(s, stagings):
        s.emit("z", BEYOND, stagings[0], s.dot(("to", "zb"), ("t_ob", "z_bb")))
        value = s.dot(("z_bo", "yo"), ("z_bb", "y_bo"))
        stagings[1][...] = s.scaled(value, s.near_present(BEYOND, rows))
        s.outs["z_new"][...] = s.load("z_sum") + s.dot(("t_ob", "z_bo"))
        s.outs["y_new"][...] = s.load("y_sum") + s.dot(("yb", stagings[1]))

    z_next, y_sum, z_sum = call(
        beyond_body,
        dict(to=to, zb=zb, t_ob=t_ob, z_bb=z_bb, z_bo=z_bo, yo=yo, y_bo=y_bo, yb=yb, y_sum=y_sum, z_sum=z_sum),
        dict(z=z_next), dict(y_new=sums, z_new=sums), 2,
    )

    def rows_z_body(s, stagings):
        s.emit("z", UPPER, stagings[0], s.dot(("to", "zp"), ("t_op", "z_pp")))
        s.emit("z", LOWER, stagings[1], s.dot(("to", "zm"), ("t_om", "z_mm")))
        s.emit("y", PARTNER, stagings[2], s.dot(("yo", "t_oa"), ("ya", "t_aa")))

    y_next, z_next = call(
        rows_z_body,
        dict(to=to, zp=zp, t_op=t_op, z_pp=z_pp, zm=zm, t_om=t_om, z_mm=z_mm, yo=yo, t_oa=t_oa, ya=ya, t_aa=t_aa),
        dict(y=y_next, z=z_next), {}, 3,
    )

    def last_body(s, stagings):
        value = s.load("a_sum") + s.dot(("z_ao", "yo"))
        stagings[3][...] = s.scaled(value, s.near_present(PARTNER, rows))
        s.emit("z", OWN, stagings[1], s.load("z_sum") + s.dot(("t_oa", "z_ao")))
        s.emit("y", OWN, stagings[2], s.load("y_sum") + s.dot(("ya", stagings[3])))
        s.emit("y", BEYOND, stagings[0], s.load("b_sum") + s.dot(("yb", "t_bb")))

    return call(
        last_body,
        dict(yo=yo, yb=yb, t_bb=t_bb, z_ao=z_ao, a_sum=a_sum, b_sum=b_sum, t_oa=t_oa, z_sum=z_sum, ya=ya, y_sum=y_sum),
        dict(y=y_next, z=z_next), {}, 4,
    )


def solution(mesh):
    spec = P(("row", "col"), None, None, None)

    return jax.shard_map(on_device, mesh=mesh, in_specs=(spec, spec, P()), out_specs=(spec, spec), check_vma=False)
```

time: 136 us -> 150 us (1.10)
  the two profiles are of different devices: /device:TPU:0 before, /device:TPU:3 now
where the time goes in v2:
time: 150 us; the launch traced here: 149 us
  waiting for transfers between devices  86.8 us (58%)
  Pallas kernels  32.7 us (22%)
  starting transfers between devices  29.1 us (19%)
    ppermute x26, waiting for transfers between devices, move(): return lax.ppermute(value, axis, route)  86.8 us
    ppermute x26, starting transfers between devices, move(): return lax.ppermute(value, axis, route)  29.1 us
    pallas_call x8, Pallas kernels, stage_call(): pl.pallas_call(kernel, out_shape=[sparse_shape] * len(sink_keys) + [outs[...  24.2 us
    pallas_call x3, Pallas kernels, pack(): pl.pallas_call(body, out_shape=[jax.ShapeDtypeStruct((order, order), bloc...  8.53 us
  transfers between devices with their start and end apart: 26, of which 10 were waited for; matrix products, arithmetic and copies ran while one was open for 0% of the time, Pallas kernels for 16%

profile of v2, /device:TPU:3, one launch (start us, length us, event | category | flops | bytes accessed | tf_op | source)
XLA Modules:
  0.0 149.5 jit_solution(13118386408130330295)
XLA Ops:
  0.6 2.7 %shard_map.50 = (bf16[512,512]{1,0:T(8,128)(2,1)S(1)}, s32[80]{0:T(128)S(1)}) custom-call(s32[16,128]{1,0:T(8,128)} %bitcast.1, bf16[4,16,128,128]{3,2,1,0:T(8,128)(2,1)} %blocks.4), custom_call_target="tpu_custom_call" | custom-call | tf_op jit(solution)/shard_map/pallas_call | solution.py:135
  3.4 2.1 %shard_map.51 = (bf16[512,512]{1,0:T(8,128)(2,1)S(1)}, bf16[512,512]{1,0:T(8,128)(2,1)S(1)}, bf16[512,512]{1,0:T(8,128)(2,1)S(1)}, bf16[512,512]{1,0:T(8,128)(2,1)S(1)}) custom-call(s32[80]{0:T(128)S(1)} %get-tuple-element.33.table.refs_10_.refs_13_.refs_8_.refs_11_.refs_7_.refs_12_, bf16[4,16,128,128]{3,2,1,0:T(8,128)(2,1)} %blocks.4), custom_call_target="tpu_custom_call" | custom-call | tf_op jit(solution)/shard_map/pallas_call | solution.py:135
  5.5 0.7 collective-permute-start.1
  6.2 1.2 collective-permute-start.2
  7.4 3.7 %shard_map.52 = (bf16[512,512]{1,0:T(8,128)(2,1)S(1)}, bf16[512,512]{1,0:T(8,128)(2,1)S(1)}, bf16[512,512]{1,0:T(8,128)(2,1)S(1)}, bf16[512,512]{1,0:T(8,128)(2,...) custom-call(s32[16,128]{1,0:T(8,128)} %bitcast.2, ...), custom_call_target="tpu_custom_call" | custom-call | tf_op jit(solution)/shard_map/pallas_call | solution.py:135
  11.1 0.3 collective-permute-start.10
  11.5 1.2 collective-permute-start.11
  12.7 0.3 collective-permute-start.3
  12.9 6.4 %collective-permute-done.10.refs_6_ = bf16[256,512]{1,0:T(8,128)(2,1)S(1)} collective-permute-done((bf16[256,512]{1,0:T(8,128)(2,1)S(1)}, bf16[256,512]{1,0:T(8,128)(2,1)S(1)}, u32[]{:S(2)}, u32[]{:S(2)}) %collective-permute-start.10) | collective-permute-done | bytes 262176 | tf_op jit(solution)/shard_map/ppermute | solution.py:269
  19.3 0.3 collective-permute-start.4
  19.6 5.3 %collective-permute-done.11.refs_7_ = bf16[256,512]{1,0:T(8,128)(2,1)S(1)} collective-permute-done((bf16[256,512]{1,0:T(8,128)(2,1)S(1)}, bf16[256,512]{1,0:T(8,128)(2,1)S(1)}, u32[]{:S(2)}, u32[]{:S(2)}) %collective-permute-start.11) | collective-permute-done | bytes 262176 | tf_op jit(solution)/shard_map/ppermute | solution.py:269
  24.9 0.8 collective-permute-start.6
  25.7 0.0 collective-permute-done.1.refs_3_
  25.7 0.9 collective-permute-start.7
  26.7 0.0 collective-permute-done.2.refs_5_.refs_6_
  26.7 0.3 collective-permute-start.8
  27.0 9.2 %collective-permute-done.3.refs_7_.refs_3_ = bf16[512,512]{1,0:T(8,128)(2,1)S(1)} collective-permute-done((bf16[512,512]{1,0:T(8,128)(2,1)S(1)}, bf16[512,512]{1,0:T(8,128)(2,1)S(1)}, u32[]{:S(2)}, u32[]{:S(2)}) %collective-permute-start.3) | collective-permute-done | bytes 524320 | tf_op jit(solution)/shard_map/ppermute | solution.py:269
  36.2 0.3 collective-permute-start.12
  36.5 10.9 %collective-permute-done.4 = bf16[512,512]{1,0:T(8,128)(2,1)S(1)} collective-permute-done((bf16[512,512]{1,0:T(8,128)(2,1)S(1)}, bf16[512,512]{1,0:T(8,128)(2,1)S(1)}, u32[]{:S(2)}, u32[]{:S(2)}) %collective-permute-start.4) | collective-permute-done | bytes 524320 | tf_op jit(solution)/shard_map/ppermute | solution.py:269
  47.4 0.8 collective-permute-start.14
  48.2 0.0 collective-permute-done.6.refs_3_
  48.2 0.9 collective-permute-start.15
  49.1 0.0 collective-permute-done.7.refs_6_
  49.1 0.9 collective-permute-start.16
  50.0 8.7 %collective-permute-done.8.refs_9_ = bf16[512,512]{1,0:T(8,128)(2,1)S(1)} collective-permute-done((bf16[512,512]{1,0:T(8,128)(2,1)S(1)}, bf16[512,512]{1,0:T(8,128)(2,1)S(1)}, u32[]{:S(2)}, u32[]{:S(2)}) %collective-permute-start.8) | collective-permute-done | bytes 524320 | tf_op jit(solution)/shard_map/ppermute | solution.py:269
  58.6 3.3 %collective-permute-start.5 = (bf16[512,512]{1,0:T(8,128)(2,1)S(1)}, bf16[512,512]{1,0:T(8,128)(2,1)S(1)}, u32[]{:S(2)}, u32[]{:S(2)}) collective-permute-start(bf16[512,512]{1,0:T(8,128)(2,1)S(1)} %collective-permute-done.4), channel_id=1, source_target_pairs={{0,2},{1,7},{2,4},{3,1},{4,6},{5,3},{6,0},{7,5},{8,10},{9,15},{10,... | collective-permute-start | bytes 1572872 | tf_op jit(solution)/shard_map/ppermute | solution.py:269
  61.9 8.0 %collective-permute-done.12 = bf16[512,512]{1,0:T(8,128)(2,1)S(1)} collective-permute-done((bf16[512,512]{1,0:T(8,128)(2,1)S(1)}, bf16[512,512]{1,0:T(8,128)(2,1)S(1)}, u32[]{:S(2)}, u32[]{:S(2)}) %collective-permute-start.12) | collective-permute-done | bytes 524320 | tf_op jit(solution)/shard_map/ppermute | solution.py:269
  69.9 1.4 collective-permute-start.17
  71.3 0.0 collective-permute-done.14.refs_0_
  71.3 3.3 %collective-permute-start.9 = (bf16[512,512]{1,0:T(8,128)(2,1)S(1)}, bf16[512,512]{1,0:T(8,128)(2,1)S(1)}, u32[]{:S(2)}, u32[]{:S(2)}) collective-permute-start(bf16[512,512]{1,0:T(8,128)(2,1)S(1)} %collective-permute-done.8.refs_9_), channel_id=1, source_target_pairs={{0,2},{1,7},{2,4},{3,1},{4,6},{5,3},{6,0},{7,5},{8,10},{9,15},{10,... | collective-permute-start | bytes 1572872 | tf_op jit(solution)/shard_map/ppermute | solution.py:269
  74.6 0.0 collective-permute-done.15.refs_2_.refs_3_
  74.6 0.2 collective-permute-start.13
  74.8 0.0 collective-permute-done.16.refs_4_
  74.8 0.1 collective-permute-start.18
  74.9 0.0 collective-permute-done.5.refs_9_.refs_5_
  74.9 1.4 collective-permute-start.19
  76.3 2.1 %shard_map.53 = (bf16[512,512]{1,0:T(8,128)(2,1)S(1)}, bf16[256,512]{1,0:T(8,128)(2,1)S(1)}, bf16[256,512]{1,0:T(8,128)(2,1)S(1)}) custom-call(bf16[512,512]{1,0:T(8,128)(2,1)S(1)} %get-tuple-element.37.refs_0_.refs_10_, bf16[512,512]{1,0:T(8,128)(2,1)S(1)} %get-tuple-element.34.refs_1_.refs_4_.refs_0_.refs_7_, ...), custom_call_target="tpu_custom_call" | custom-call | tf_op jit(solution)/shard_map/pallas_call | solution.py:244
  78.3 0.0 collective-permute-done.17.refs_5_.refs_6_
  78.3 0.1 collective-permute-start
  78.4 24.7 %collective-permute-done.18.refs_9_ = bf16[256,512]{1,0:T(8,128)(2,1)S(1)} collective-permute-done((bf16[256,512]{1,0:T(8,128)(2,1)S(1)}, bf16[256,512]{1,0:T(8,128)(2,1)S(1)}, u32[]{:S(2)}, u32[]{:S(2)}) %collective-permute-start.18) | collective-permute-done | bytes 262176 | tf_op jit(solution)/shard_map/ppermute | solution.py:269
  103.2 0.0 collective-permute-start.24
  103.2 5.3 %collective-permute-done.19.refs_10_ = bf16[256,512]{1,0:T(8,128)(2,1)S(1)} collective-permute-done((bf16[256,512]{1,0:T(8,128)(2,1)S(1)}, bf16[256,512]{1,0:T(8,128)(2,1)S(1)}, u32[]{:S(2)}, u32[]{:S(2)}) %collective-permute-start.19) | collective-permute-done | bytes 262176 | tf_op jit(solution)/shard_map/ppermute | solution.py:269
  108.5 1.2 collective-permute-start.25
  109.6 0.0 collective-permute-done.9.refs_12_
  109.6 1.0 collective-permute-start.20
  110.6 0.0 collective-permute-done.13.refs_3_
  110.6 0.5 collective-permute-start.22
  111.1 6.9 %collective-permute-done.20.refs_10_ = bf16[256,512]{1,0:T(8,128)(2,1)S(1)} collective-permute-done((bf16[256,512]{1,0:T(8,128)(2,1)S(1)}, bf16[256,512]{1,0:T(8,128)(2,1)S(1)}, u32[]{:S(2)}, u32[]{:S(2)}) %collective-permute-start.20) | collective-permute-done | bytes 262176 | tf_op jit(solution)/shard_map/ppermute | solution.py:269
  118.0 4.0 %collective-permute-start.21 = (bf16[256,512]{1,0:T(8,128)(2,1)S(1)}, bf16[256,512]{1,0:T(8,128)(2,1)S(1)}, u32[]{:S(2)}, u32[]{:S(2)}) collective-permute-start(bf16[256,512]{1,0:T(8,128)(2,1)S(1)} %collective-permute-done.20.refs_10_), channel_id=1, source_target_pairs={{0,2},{1,7},{2,4},{3,1},{4,6},{5,3},{6,0},{7,5},{8,10},{9,15},{10,... | collective-permute-start | bytes 786440 | tf_op jit(solution)/shard_map/ppermute | solution.py:269
  122.0 1.4 collective-permute-done.22.refs_11_
  123.4 3.7 %collective-permute-start.23 = (bf16[256,512]{1,0:T(8,128)(2,1)S(1)}, bf16[256,512]{1,0:T(8,128)(2,1)S(1)}, u32[]{:S(2)}, u32[]{:S(2)}) collective-permute-start(bf16[256,512]{1,0:T(8,128)(2,1)S(1)} %collective-permute-done.22.refs_11_), channel_id=1, source_target_pairs={{0,2},{1,7},{2,4},{3,1},{4,6},{5,3},{6,0},{7,5},{8,10},{9,15},{10,... | collective-permute-start | bytes 786440 | tf_op jit(solution)/shard_map/ppermute | solution.py:269
  127.1 2.9 %shard_map.54 = (bf16[512,512]{1,0:T(8,128)(2,1)S(1)}, bf16[512,512]{1,0:T(8,128)(2,1)S(1)}, bf16[512,512]{1,0:T(8,128)(2,1)S(1)}, bf16[512,512]{1,0:T(8,128)(2,1)S(1)}) custom-call(bf16[512,512]{1,0:T(8,128)(2,1)S(1)} %get-tuple-element.37.refs_0_.refs_10_, bf16[512,512]{1,0:T(8,128)(2,1)S(1)} %get-tuple-element.41.refs_1_.refs_8_.refs_2_, ...), custom_call_target="tpu_custom_call" | custom-call | tf_op jit(solution)/shard_map/pallas_call | solution.py:244
  130.0 2.5 %shard_map.55 = (bf16[4,16,128,128]{3,2,1,0:T(8,128)(2,1)}, f32[512,512]{1,0:T(8,128)S(1)}, f32[512,512]{1,0:T(8,128)S(1)}) custom-call(bf16[512,512]{1,0:T(8,128)(2,1)S(1)} %get-tuple-element.45.refs_0_.refs_7_, bf16[512,512]{1,0:T(8,128)(2,1)S(1)} %get-tuple-element.36.refs_6_.refs_8_.refs_1_, ...), custom_call_target="tpu_custom_call" | custom-call | tf_op jit(solution)/shard_map/pallas_call | solution.py:244
  132.5 3.7 %shard_map.56 = (f32[512,512]{1,0:T(8,128)S(1)}, f32[512,512]{1,0:T(8,128)S(1)}) custom-call(bf16[512,512]{1,0:T(8,128)(2,1)S(1)} %collective-permute-done.14.refs_0_, bf16[512,512]{1,0:T(8,128)(2,1)S(1)} %get-tuple-element.34.refs_1_.refs_4_.refs_0_.refs_7_, bf16[512,512]{1,0:T(8,128)(2,1)S(1)} %collective-permute-done.15.refs_2_.refs_3_, ...), custom_call_target="tpu_custom_call" | custom-call | tf_op jit(solution)/shard_map/pallas_call | solution.py:244
  136.2 3.3 %shard_map.57 = (bf16[4,16,128,128]{3,2,1,0:T(8,128)(2,1)}, f32[512,512]{1,0:T(8,128)S(1)}, f32[512,512]{1,0:T(8,128)S(1)}) custom-call(bf16[512,512]{1,0:T(8,128)(2,1)S(1)} %get-tuple-element.45.refs_0_.refs_7_, bf16[512,512]{1,0:T(8,128)(2,1)S(1)} %get-tuple-element.43.refs_8_.refs_11_.refs_1_, ...), custom_call_target="tpu_custom_call", output_to_operand_aliasing={{0}: (13, {})} | custom-call | tf_op jit(solution)/shard_map/pallas_call | solution.py:244
  139.5 0.0 collective-permute-done.24.refs_3_
  139.5 0.0 collective-permute-done.25.refs_6_
  139.5 2.8 %shard_map.58.refs_14_ = bf16[4,16,128,128]{3,2,1,0:T(8,128)(2,1)} custom-call(bf16[512,512]{1,0:T(8,128)(2,1)S(1)} %get-tuple-element.34.refs_1_.refs_4_.refs_0_.refs_7_, bf16[512,512]{1,0:T(8,128)(2,1)S(1)} %get-tuple-element.52.refs_11_.refs_1_.refs_2_, bf16[512,512]{1,0:T(8,128)(2,1)S(1)} %get-tuple-element.41.refs_1_.refs_8_.refs_2_, ...), custom_call_target="tpu_custom_call" | custom-call | tf_op jit(solution)/shard_map/pallas_call | solution.py:244
  142.4 3.7 %shard_map.59 = (bf16[4,16,128,128]{3,2,1,0:T(8,128)(2,1)}, bf16[4,16,128,128]{3,2,1,0:T(8,128)(2,1)}) custom-call(bf16[512,512]{1,0:T(8,128)(2,1)S(1)} %get-tuple-element.45.refs_0_.refs_7_, bf16[512,512]{1,0:T(8,128)(2,1)S(1)} %get-tuple-element.38.refs_2_.refs_1_, ...), custom_call_target="tpu_custom_call", output_to_operand_aliasing={{0}: (14, {}), {1}: (15, {})} | custom-call | tf_op jit(solution)/shard_map/pallas_call | solution.py:244
  146.0 0.0 collective-permute-done.refs_2_
  146.0 0.0 collective-permute-done.21.refs_9_
  146.1 0.0 collective-permute-done.23.refs_10_
  146.1 3.3 %shard_map.60 = (bf16[4,16,128,128]{3,2,1,0:T(8,128)(2,1)}, bf16[4,16,128,128]{3,2,1,0:T(8,128)(2,1)}) custom-call(bf16[512,512]{1,0:T(8,128)(2,1)S(1)} %get-tuple-element.34.refs_1_.refs_4_.refs_0_.refs_7_, bf16[512,512]{1,0:T(8,128)(2,1)S(1)} %get-tuple-element.35.refs_10_.refs_6_.refs_1_, ...), custom_call_target="tpu_custom_call", output_to_operand_aliasing={{0}: (13, {}), {1}: (14, {})} | custom-call | tf_op jit(solution)/shard_map/pallas_call | solution.py:244
Async XLA Ops:
  5.5 20.3 %collective-permute-start.1 = (bf16[512,512]{1,0:T(8,128)(2,1)S(1)}, bf16[512,512]{1,0:T(8,128)(2,1)S(1)}, u32[]{:S(2)}, u32[]{:S(2)}) collective-permute-start(bf16[512,512]{1,0:T(8,128)(2,1)S(1)} %get-tuple-element.39.refs_4_.refs_9_.refs_5_), channel_id=1, source_target_pairs={{0,24},{8,0},{16,8},{24,16},{1,25},{9,1},{17,9},{25,17},{2,26},{10... | collective-permute-start | bytes 1572872 | tf_op jit(solution)/shard_map/ppermute | solution.py:269
  6.2 20.5 %collective-permute-start.2 = (bf16[512,512]{1,0:T(8,128)(2,1)S(1)}, bf16[512,512]{1,0:T(8,128)(2,1)S(1)}, u32[]{:S(2)}, u32[]{:S(2)}) collective-permute-start(bf16[512,512]{1,0:T(8,128)(2,1)S(1)} %get-tuple-element.41.refs_1_.refs_8_.refs_2_), channel_id=1, source_target_pairs={{0,8},{8,16},{16,24},{24,0},{1,9},{9,17},{17,25},{25,1},{2,10},{10... | collective-permute-start | bytes 1572872 | tf_op jit(solution)/shard_map/ppermute | solution.py:269
  11.1 8.2 %collective-permute-start.10 = (bf16[256,512]{1,0:T(8,128)(2,1)S(1)}, bf16[256,512]{1,0:T(8,128)(2,1)S(1)}, u32[]{:S(2)}, u32[]{:S(2)}) collective-permute-start(bf16[256,512]{1,0:T(8,128)(2,1)S(1)} %get-tuple-element.48), channel_id=1, source_target_pairs={{0,1},{1,0},{2,3},{3,2},{4,5},{5,4},{6,7},{7,6},{8,9},{9,8},{10,11... | collective-permute-start | bytes 786440 | tf_op jit(solution)/shard_map/ppermute | solution.py:269
  11.5 13.4 %collective-permute-start.11 = (bf16[256,512]{1,0:T(8,128)(2,1)S(1)}, bf16[256,512]{1,0:T(8,128)(2,1)S(1)}, u32[]{:S(2)}, u32[]{:S(2)}) collective-permute-start(bf16[256,512]{1,0:T(8,128)(2,1)S(1)} %get-tuple-element.49), channel_id=1, source_target_pairs={{0,1},{1,0},{2,3},{3,2},{4,5},{5,4},{6,7},{7,6},{8,9},{9,8},{10,11... | collective-permute-start | bytes 786440 | tf_op jit(solution)/shard_map/ppermute | solution.py:269
  12.7 23.5 %collective-permute-start.3 = (bf16[512,512]{1,0:T(8,128)(2,1)S(1)}, bf16[512,512]{1,0:T(8,128)(2,1)S(1)}, u32[]{:S(2)}, u32[]{:S(2)}) collective-permute-start(bf16[512,512]{1,0:T(8,128)(2,1)S(1)} %get-tuple-element.42.refs_7_.refs_9_), channel_id=1, source_target_pairs={{0,1},{1,0},{2,3},{3,2},{4,5},{5,4},{6,7},{7,6},{8,9},{9,8},{10,11... | collective-permute-start | bytes 1572872 | tf_op jit(solution)/shard_map/ppermute | solution.py:269
  19.3 28.1 %collective-permute-start.4 = (bf16[512,512]{1,0:T(8,128)(2,1)S(1)}, bf16[512,512]{1,0:T(8,128)(2,1)S(1)}, u32[]{:S(2)}, u32[]{:S(2)}) collective-permute-start(bf16[512,512]{1,0:T(8,128)(2,1)S(1)} %get-tuple-element.35.refs_10_.refs_6_.refs_1_), channel_id=1, source_target_pairs={{0,1},{1,0},{2,3},{3,2},{4,5},{5,4},{6,7},{7,6},{8,9},{9,8},{10,11... | collective-permute-start | bytes 1572872 | tf_op jit(solution)/shard_map/ppermute | solution.py:269
  24.9 23.3 %collective-permute-start.6 = (bf16[512,512]{1,0:T(8,128)(2,1)S(1)}, bf16[512,512]{1,0:T(8,128)(2,1)S(1)}, u32[]{:S(2)}, u32[]{:S(2)}) collective-permute-start(bf16[512,512]{1,0:T(8,128)(2,1)S(1)} %get-tuple-element.34.refs_1_.refs_4_.refs_0_.refs_7_), channel_id=1, source_target_pairs={{0,24},{8,0},{16,8},{24,16},{1,25},{9,1},{17,9},{25,17},{2,26},{10... | collective-permute-start | bytes 1572872 | tf_op jit(solution)/shard_map/ppermute | solution.py:269
  25.7 23.4 %collective-permute-start.7 = (bf16[512,512]{1,0:T(8,128)(2,1)S(1)}, bf16[512,512]{1,0:T(8,128)(2,1)S(1)}, u32[]{:S(2)}, u32[]{:S(2)}) collective-permute-start(bf16[512,512]{1,0:T(8,128)(2,1)S(1)} %get-tuple-element.34.refs_1_.refs_4_.refs_0_.refs_7_), channel_id=1, source_target_pairs={{0,8},{8,16},{16,24},{24,0},{1,9},{9,17},{17,25},{25,1},{2,10},{10... | collective-permute-start | bytes 1572872 | tf_op jit(solution)/shard_map/ppermute | solution.py:269
  26.7 32.0 %collective-permute-start.8 = (bf16[512,512]{1,0:T(8,128)(2,1)S(1)}, bf16[512,512]{1,0:T(8,128)(2,1)S(1)}, u32[]{:S(2)}, u32[]{:S(2)}) collective-permute-start(bf16[512,512]{1,0:T(8,128)(2,1)S(1)} %get-tuple-element.34.refs_1_.refs_4_.refs_0_.refs_7_), channel_id=1, source_target_pairs={{0,1},{1,0},{2,3},{3,2},{4,5},{5,4},{6,7},{7,6},{8,9},{9,8},{10,11... | collective-permute-start | bytes 1572872 | tf_op jit(solution)/shard_map/ppermute | solution.py:269
  36.2 33.7 %collective-permute-start.12 = (bf16[512,512]{1,0:T(8,128)(2,1)S(1)}, bf16[512,512]{1,0:T(8,128)(2,1)S(1)}, u32[]{:S(2)}, u32[]{:S(2)}) collective-permute-start(bf16[512,512]{1,0:T(8,128)(2,1)S(1)} %get-tuple-element.43.refs_8_.refs_11_.refs_1_), channel_id=1, source_target_pairs={{0,1},{1,0},{2,3},{3,2},{4,5},{5,4},{6,7},{7,6},{8,9},{9,8},{10,11... | collective-permute-start | bytes 1572872 | tf_op jit(solution)/shard_map/ppermute | solution.py:269
  47.4 23.9 %collective-permute-start.14 = (bf16[512,512]{1,0:T(8,128)(2,1)S(1)}, bf16[512,512]{1,0:T(8,128)(2,1)S(1)}, u32[]{:S(2)}, u32[]{:S(2)}) collective-permute-start(bf16[512,512]{1,0:T(8,128)(2,1)S(1)} %get-tuple-element.40.refs_4_.refs_5_), channel_id=1, source_target_pairs={{0,24},{8,0},{16,8},{24,16},{1,25},{9,1},{17,9},{25,17},{2,26},{10... | collective-permute-start | bytes 1572872 | tf_op jit(solution)/shard_map/ppermute | solution.py:269
  48.2 26.3 %collective-permute-start.15 = (bf16[512,512]{1,0:T(8,128)(2,1)S(1)}, bf16[512,512]{1,0:T(8,128)(2,1)S(1)}, u32[]{:S(2)}, u32[]{:S(2)}) collective-permute-start(bf16[512,512]{1,0:T(8,128)(2,1)S(1)} %get-tuple-element.37.refs_0_.refs_10_), channel_id=1, source_target_pairs={{0,24},{8,0},{16,8},{24,16},{1,25},{9,1},{17,9},{25,17},{2,26},{10... | collective-permute-start | bytes 1572872 | tf_op jit(solution)/shard_map/ppermute | solution.py:269
  49.1 25.7 %collective-permute-start.16 = (bf16[512,512]{1,0:T(8,128)(2,1)S(1)}, bf16[512,512]{1,0:T(8,128)(2,1)S(1)}, u32[]{:S(2)}, u32[]{:S(2)}) collective-permute-start(bf16[512,512]{1,0:T(8,128)(2,1)S(1)} %get-tuple-element.38.refs_2_.refs_1_), channel_id=1, source_target_pairs={{0,8},{8,16},{16,24},{24,0},{1,9},{9,17},{17,25},{25,1},{2,10},{10... | collective-permute-start | bytes 1572872 | tf_op jit(solution)/shard_map/ppermute | solution.py:269
  58.6 16.2 %collective-permute-start.5 = (bf16[512,512]{1,0:T(8,128)(2,1)S(1)}, bf16[512,512]{1,0:T(8,128)(2,1)S(1)}, u32[]{:S(2)}, u32[]{:S(2)}) collective-permute-start(bf16[512,512]{1,0:T(8,128)(2,1)S(1)} %collective-permute-done.4), channel_id=1, source_target_pairs={{0,2},{1,7},{2,4},{3,1},{4,6},{5,3},{6,0},{7,5},{8,10},{9,15},{10,... | collective-permute-start | bytes 1572872 | tf_op jit(solution)/shard_map/ppermute | solution.py:269
  69.9 8.5 %collective-permute-start.17 = (bf16[512,512]{1,0:T(8,128)(2,1)S(1)}, bf16[512,512]{1,0:T(8,128)(2,1)S(1)}, u32[]{:S(2)}, u32[]{:S(2)}) collective-permute-start(bf16[512,512]{1,0:T(8,128)(2,1)S(1)} %get-tuple-element.37.refs_0_.refs_10_), channel_id=1, source_target_pairs={{0,8},{8,16},{16,24},{24,0},{1,9},{9,17},{17,25},{25,1},{2,10},{10... | collective-permute-start | bytes 1572872 | tf_op jit(solution)/shard_map/ppermute | solution.py:269
  71.3 38.4 %collective-permute-start.9 = (bf16[512,512]{1,0:T(8,128)(2,1)S(1)}, bf16[512,512]{1,0:T(8,128)(2,1)S(1)}, u32[]{:S(2)}, u32[]{:S(2)}) collective-permute-start(bf16[512,512]{1,0:T(8,128)(2,1)S(1)} %collective-permute-done.8.refs_9_), channel_id=1, source_target_pairs={{0,2},{1,7},{2,4},{3,1},{4,6},{5,3},{6,0},{7,5},{8,10},{9,15},{10,... | collective-permute-start | bytes 1572872 | tf_op jit(solution)/shard_map/ppermute | solution.py:269
  74.6 36.1 %collective-permute-start.13 = (bf16[512,512]{1,0:T(8,128)(2,1)S(1)}, bf16[512,512]{1,0:T(8,128)(2,1)S(1)}, u32[]{:S(2)}, u32[]{:S(2)}) collective-permute-start(bf16[512,512]{1,0:T(8,128)(2,1)S(1)} %collective-permute-done.12), channel_id=1, source_target_pairs={{0,2},{1,7},{2,4},{3,1},{4,6},{5,3},{6,0},{7,5},{8,10},{9,15},{10,... | collective-permute-start | bytes 1572872 | tf_op jit(solution)/shard_map/ppermute | solution.py:269
  74.8 28.4 %collective-permute-start.18 = (bf16[256,512]{1,0:T(8,128)(2,1)S(1)}, bf16[256,512]{1,0:T(8,128)(2,1)S(1)}, u32[]{:S(2)}, u32[]{:S(2)}) collective-permute-start(bf16[256,512]{1,0:T(8,128)(2,1)S(1)} %collective-permute-done.10.refs_6_), channel_id=1, source_target_pairs={{0,2},{1,7},{2,4},{3,1},{4,6},{5,3},{6,0},{7,5},{8,10},{9,15},{10,... | collective-permute-start | bytes 786440 | tf_op jit(solution)/shard_map/ppermute | solution.py:269
  74.9 33.6 %collective-permute-start.19 = (bf16[256,512]{1,0:T(8,128)(2,1)S(1)}, bf16[256,512]{1,0:T(8,128)(2,1)S(1)}, u32[]{:S(2)}, u32[]{:S(2)}) collective-permute-start(bf16[256,512]{1,0:T(8,128)(2,1)S(1)} %collective-permute-done.11.refs_7_), channel_id=1, source_target_pairs={{0,2},{1,7},{2,4},{3,1},{4,6},{5,3},{6,0},{7,5},{8,10},{9,15},{10,... | collective-permute-start | bytes 786440 | tf_op jit(solution)/shard_map/ppermute | solution.py:269
  78.3 67.7 %collective-permute-start = (bf16[512,512]{1,0:T(8,128)(2,1)S(1)}, bf16[512,512]{1,0:T(8,128)(2,1)S(1)}, u32[]{:S(2)}, u32[]{:S(2)}) collective-permute-start(bf16[512,512]{1,0:T(8,128)(2,1)S(1)} %get-tuple-element.36.refs_6_.refs_8_.refs_1_), channel_id=1, source_target_pairs={{0,1},{1,0},{2,3},{3,2},{4,5},{5,4},{6,7},{7,6},{8,9},{9,8},{10,11... | collective-permute-start | bytes 1572872 | tf_op jit(solution)/shard_map/ppermute | solution.py:269
  103.2 36.3 %collective-permute-start.24 = (bf16[512,512]{1,0:T(8,128)(2,1)S(1)}, bf16[512,512]{1,0:T(8,128)(2,1)S(1)}, u32[]{:S(2)}, u32[]{:S(2)}) collective-permute-start(bf16[512,512]{1,0:T(8,128)(2,1)S(1)} %get-tuple-element.45.refs_0_.refs_7_), channel_id=1, source_target_pairs={{0,24},{8,0},{16,8},{24,16},{1,25},{9,1},{17,9},{25,17},{2,26},{10... | collective-permute-start | bytes 1572872 | tf_op jit(solution)/shard_map/ppermute | solution.py:269
  108.5 31.0 %collective-permute-start.25 = (bf16[512,512]{1,0:T(8,128)(2,1)S(1)}, bf16[512,512]{1,0:T(8,128)(2,1)S(1)}, u32[]{:S(2)}, u32[]{:S(2)}) collective-permute-start(bf16[512,512]{1,0:T(8,128)(2,1)S(1)} %get-tuple-element.45.refs_0_.refs_7_), channel_id=1, source_target_pairs={{0,8},{8,16},{16,24},{24,0},{1,9},{9,17},{17,25},{25,1},{2,10},{10... | collective-permute-start | bytes 1572872 | tf_op jit(solution)/shard_map/ppermute | solution.py:269
  109.6 8.3 %collective-permute-start.20 = (bf16[256,512]{1,0:T(8,128)(2,1)S(1)}, bf16[256,512]{1,0:T(8,128)(2,1)S(1)}, u32[]{:S(2)}, u32[]{:S(2)}) collective-permute-start(bf16[256,512]{1,0:T(8,128)(2,1)S(1)} %get-tuple-element.59), channel_id=1, source_target_pairs={{0,1},{1,0},{2,3},{3,2},{4,5},{5,4},{6,7},{7,6},{8,9},{9,8},{10,11... | collective-permute-start | bytes 786440 | tf_op jit(solution)/shard_map/ppermute | solution.py:269
  110.6 12.8 %collective-permute-start.22 = (bf16[256,512]{1,0:T(8,128)(2,1)S(1)}, bf16[256,512]{1,0:T(8,128)(2,1)S(1)}, u32[]{:S(2)}, u32[]{:S(2)}) collective-permute-start(bf16[256,512]{1,0:T(8,128)(2,1)S(1)} %get-tuple-element.60), channel_id=1, source_target_pairs={{0,1},{1,0},{2,3},{3,2},{4,5},{5,4},{6,7},{7,6},{8,9},{9,8},{10,11... | collective-permute-start | bytes 786440 | tf_op jit(solution)/shard_map/ppermute | solution.py:269
  118.0 28.1 %collective-permute-start.21 = (bf16[256,512]{1,0:T(8,128)(2,1)S(1)}, bf16[256,512]{1,0:T(8,128)(2,1)S(1)}, u32[]{:S(2)}, u32[]{:S(2)}) collective-permute-start(bf16[256,512]{1,0:T(8,128)(2,1)S(1)} %collective-permute-done.20.refs_10_), channel_id=1, source_target_pairs={{0,2},{1,7},{2,4},{3,1},{4,6},{5,3},{6,0},{7,5},{8,10},{9,15},{10,... | collective-permute-start | bytes 786440 | tf_op jit(solution)/shard_map/ppermute | solution.py:269
  123.4 22.7 %collective-permute-start.23 = (bf16[256,512]{1,0:T(8,128)(2,1)S(1)}, bf16[256,512]{1,0:T(8,128)(2,1)S(1)}, u32[]{:S(2)}, u32[]{:S(2)}) collective-permute-start(bf16[256,512]{1,0:T(8,128)(2,1)S(1)} %collective-permute-done.22.refs_11_), channel_id=1, source_target_pairs={{0,2},{1,7},{2,4},{3,1},{4,6},{5,3},{6,0},{7,5},{8,10},{9,15},{10,... | collective-permute-start | bytes 786440 | tf_op jit(solution)/shard_map/ppermute | solution.py:269
